TPU v7x, 32 devices: a whole 2x2x4 slice. The times are simulated.
32 devices in a mesh: fsdp: 4 (over x, core), ctx: 8 (over z, y).
Axes of the slice: x: 2, y: 2, z: 4, core: 2. Of those that a mesh axis runs over, the one named last changes fastest.
Arguments:
- queries: bfloat16 [4, 3072, 2560], P('fsdp', 'ctx'), may hold values from -2 to 2
- keys_rot: bfloat16 [4, 3072, 512], P('fsdp', 'ctx'), may hold values from -1 to 1
- values: bfloat16 [4, 3072, 512], P('fsdp', 'ctx'), may hold values from -6 to 6
- attention_out: bfloat16 [4, 3072, 2560], P('fsdp', 'ctx'), may hold values from -6 to 6
- grad_out: bfloat16 [4, 3072, 2560], P('fsdp', 'ctx'), may hold values from -6 to 6
- layer_input: bfloat16 [4, 3072, 2560], P('fsdp', 'ctx'), may hold values from -6 to 6
- doc_lengths: int32 [4, 7], P('fsdp'), may hold values from 1 to 768, 3072 in all within a row
Outputs:
- grad_query: bfloat16 [4, 3072, 2560], P('fsdp', 'ctx')
- grad_wk: float32 [2560, 512], P('ctx', 'fsdp')
- grad_wv: float32 [2560, 512], P('ctx', 'fsdp')
Inputs may be any that keep to these rules, and one draw needn't show every extreme that they name: `doc_lengths`: each row holds the lengths of the documents of one sequence in order; they sum to 3072, and the longest is exactly 768.
All inputs are finite; a program needn't handle non-finite values.
Results may differ from a plain program's by a relative error of at most 0.0049.
Values may be sent and summed in bfloat16 or wider, within the bound.
A program may use at most 128 MiB of HBM per device.

v0:
```python
import math

import jax
import jax.numpy as jnp
from jax import lax
from jax.sharding import PartitionSpec as P

H = 20
G = 4
HD = 128
DW = 2560
SPAN = 2


def passed_along(x, axis, by):
    peers = lax.axis_size(axis)
    pairs = [(i, i + by) for i in range(peers) if 0 <= i + by < peers]
    return lax.ppermute(x, axis, pairs)


def rope_back(grad_rows, places):
    count = grad_rows.shape[0]
    split = grad_rows.reshape(count, -1, HD)
    halfway = HD // 2
    inverse_freq = jnp.power(
        jnp.float32(1000000.0), -(jnp.arange(halfway, dtype=jnp.float32) * 2.0 / HD)
    )
    angles = places.astype(jnp.float32)[:, None] * inverse_freq[None, :]
    cosine = jnp.cos(angles)[:, None, :]
    sine = jnp.sin(angles)[:, None, :]
    first = split[..., :halfway]
    second = split[..., halfway:]
    return jnp.concatenate(
        [first * cosine + second * sine, second * cosine - first * sine], axis=-1
    ).reshape(count, -1)


def group_scores(q_group, k_group):
    return jnp.einsum("trd,sd->rts", q_group, k_group, preferred_element_type=jnp.float32) * (
        1.0 / math.sqrt(HD)
    )


def exp_totals(logit_matrix, allowed):
    return jnp.sum(jnp.where(allowed[None], jnp.exp(logit_matrix), 0.0), axis=-1)


def group_grads(logit_matrix, allowed, log_total, q_group, d_group, dots_group, k_group, v_group):
    softmax_scale = 1.0 / math.sqrt(HD)
    probs = jnp.where(allowed[None], jnp.exp(logit_matrix - log_total[..., None]), 0.0)
    probability_narrow = probs.astype(jnp.bfloat16)
    probability_gradient = jnp.einsum(
        "trd,sd->rts", d_group, v_group, preferred_element_type=jnp.float32
    )
    logit_gradient = (probs * (probability_gradient - dots_group[..., None])).astype(jnp.bfloat16)
    dv_part = jnp.einsum(
        "rts,trd->sd", probability_narrow, d_group, preferred_element_type=jnp.float32
    )
    dk_part = (
        jnp.einsum("rts,trd->sd", logit_gradient, q_group, preferred_element_type=jnp.float32)
        * softmax_scale
    )
    dq_part = (
        jnp.einsum("rts,sd->trd", logit_gradient, k_group, preferred_element_type=jnp.float32)
        * softmax_scale
    )
    return (dq_part, dk_part, dv_part)


def on_device(queries, keys_rot, values, attention_out, grad_out, layer_input, doc_lengths):
    q_rows = queries[0]
    k_rows = keys_rot[0]
    v_rows = values[0]
    d_rows = grad_out[0]
    inputs = layer_input[0]
    lengths = doc_lengths[0]
    rows_here = q_rows.shape[0]
    repeat = H // G
    shard_index = lax.axis_index("ctx")
    q_place = shard_index * rows_here + jnp.arange(rows_here, dtype=jnp.int32)
    starts = jnp.cumsum(lengths) - lengths
    q_start = jnp.max(jnp.where(starts[None, :] <= q_place[:, None], starts[None, :], 0), axis=1)
    row_dots = jnp.sum(
        (attention_out[0].astype(jnp.float32) * d_rows.astype(jnp.float32)).reshape(
            rows_here, G, repeat, HD
        ),
        axis=-1,
    )
    q_heads = q_rows.reshape(rows_here, G, repeat, HD)
    d_heads = d_rows.reshape(rows_here, G, repeat, HD)
    key_pieces = [k_rows]
    value_pieces = [v_rows]
    for reach in range(1, SPAN + 1):
        far_k, far_v = passed_along((k_rows, v_rows), "ctx", reach)
        key_pieces.append(far_k)
        value_pieces.append(far_v)

    def pick_group(group_id):
        q_group = lax.dynamic_index_in_dim(q_heads, group_id, 1, False)
        d_group = lax.dynamic_index_in_dim(d_heads, group_id, 1, False)
        dots_group = jnp.transpose(lax.dynamic_index_in_dim(row_dots, group_id, 1, False))
        return (q_group, d_group, dots_group)

    def key_group(rows, group_id):
        return lax.dynamic_index_in_dim(rows.reshape(rows.shape[0], G, HD), group_id, 1, False)

    width = (SPAN + 1) * rows_here
    k_window = jnp.concatenate([key_pieces[r] for r in range(SPAN, -1, -1)], axis=0)
    v_window = jnp.concatenate([value_pieces[r] for r in range(SPAN, -1, -1)], axis=0)
    k_place = (shard_index - SPAN) * rows_here + jnp.arange(width, dtype=jnp.int32)
    allowed = (k_place[None, :] >= q_start[:, None]) & (k_place[None, :] <= q_place[:, None])

    def per_group(group_id):
        q_group, d_group, dots_group = pick_group(group_id)
        k_group = key_group(k_window, group_id)
        v_group = key_group(v_window, group_id)
        logit_matrix = group_scores(q_group, k_group)
        log_total = jnp.log(exp_totals(logit_matrix, allowed))
        return group_grads(
            logit_matrix, allowed, log_total, q_group, d_group, dots_group, k_group, v_group
        )

    dq_groups, dk_groups, dv_groups = lax.map(per_group, jnp.arange(G, dtype=jnp.int32))
    dk_window = jnp.transpose(dk_groups, (1, 0, 2)).reshape(width, G * HD)
    dv_window = jnp.transpose(dv_groups, (1, 0, 2)).reshape(width, G * HD)
    dk_list = [
        dk_window[(SPAN - r) * rows_here : (SPAN - r + 1) * rows_here] for r in range(SPAN + 1)
    ]
    dv_list = [
        dv_window[(SPAN - r) * rows_here : (SPAN - r + 1) * rows_here] for r in range(SPAN + 1)
    ]
    own_dk = dk_list[0]
    own_dv = dv_list[0]
    for reach in range(1, SPAN + 1):
        back_k, back_v = (
            passed_along(dk_list[reach].astype(jnp.bfloat16), "ctx", -reach).astype(jnp.float32),
            passed_along(dv_list[reach].astype(jnp.bfloat16), "ctx", -reach).astype(jnp.float32),
        )
        own_dk = own_dk + back_k
        own_dv = own_dv + back_v
    local = q_place - q_start
    grad_rot = jnp.transpose(dq_groups, (1, 0, 2, 3)).reshape(rows_here, H * HD)
    grad_q = rope_back(grad_rot, local).astype(jnp.bfloat16)
    key_pre = rope_back(own_dk, local).astype(jnp.bfloat16)
    value_low = own_dv.astype(jnp.bfloat16)
    both_grads = jnp.concatenate([key_pre, value_low], axis=1)
    columns = G * HD
    row_count = DW // lax.axis_size("ctx")
    term = lax.dot_general(
        inputs, both_grads, (((0,), (0,)), ((), ())), preferred_element_type=jnp.float32
    )
    summed = lax.psum_scatter(
        term.reshape(lax.axis_size("ctx") * row_count, 2, columns),
        "ctx",
        scatter_dimension=0,
        tiled=True,
    )
    summed = lax.psum_scatter(summed, "fsdp", scatter_dimension=2, tiled=True)
    return (grad_q[None], summed[:, 0, :], summed[:, 1, :])


def solution(mesh):
    in_specs = (
        P("fsdp", "ctx", None),
        P("fsdp", "ctx", None),
        P("fsdp", "ctx", None),
        P("fsdp", "ctx", None),
        P("fsdp", "ctx", None),
        P("fsdp", "ctx", None),
        P("fsdp", None),
    )
    out_specs = (P("fsdp", "ctx", None), P("ctx", "fsdp"), P("ctx", "fsdp"))
    return jax.shard_map(
        on_device, mesh=mesh, in_specs=in_specs, out_specs=out_specs, check_vma=False
    )
```

profile of v0, /device:TPU:0, one launch (start us, length us, event | category | flops | bytes accessed | tf_op | source)
XLA Modules:
  0.0 443.9 jit_solution(11935030587165379807)
XLA Ops:
  7.2 5.8 %collective-permute-start.1 = (bf16[384,512]{1,0:T(8,128)(2,1)}, bf16[384,512]{1,0:T(8,128)(2,1)}, u32[]{:S(2)}, u32[]{:S(2)}) collective-permute-start(bf16[384,512]{1,0:T(8,128)(2,1)} %bitcast.192), channel_id=1, source_target_pairs={{0,1},{1,2},{2,3},{3,4},{4,5},{5,6},{6,7},{8,9},{9,10},{10,11},{11... | collective-permute-start | bytes 1179656 | tf_op jit(solution)/shard_map/ppermute | solution.py:18
  13.0 3.5 collective-permute-start
  16.5 3.4 collective-permute-start.3
  19.9 3.5 collective-permute-start.2
  24.9 3.9 copy.36
  28.8 4.0 copy.35
  37.5 3.9 copy.34
  50.4 121.2 %while.16 = (s32[]{:T(128)}, f32[4,384,5,128]{1,3,2,0:T(8,128)}, f32[4,1152,128]{1,2,0:T(8,128)}, f32[4,1152,128]{1,2,0:T(8,128)}, bf16[1152,512]{1,0:T(8,128)(2...) while((s32[]{:T(128)}, f32[4,384,5,128]{1,3,2,0:T(8,128)}, ...), condition=%wide.wide.region_5.6_spmd.clone, body=%wide.wide.region_3.5_spmd.clone.sunk | while | flops 3419016192 | bytes 86490384 | solution.py:123
  57.1 9.6 %fusion.109 = f32[5,384,1152]{1,2,0:T(8,128)} fusion(pred[384,1152]{0,1:T(8,128)(4,1)} %compare_and_fusion.3, bf16[384,4,5,128]{0,3,2,1:T(8,128)(2,1)} %get-tuple-element.360, s32[]{:T(128)S(6)} %select_n.41, bf16[1152,1,128]{2,1,0:T(2,128)(2,1)S(1)} %get-tuple-element.316), kind=kOutput, calls=%fused_computation.4.clone.clone.1 | convolution fusion | flops 1143524352 | bytes 11895808 | tf_op jit(solution)/shard_map/while/body/eval_jaxpr/reduce_sum | solution.py:45
  66.7 5.9 %fusion.113 = f32[4,1152,128]{1,2,0:T(8,128)} fusion(f32[4,1152,128]{1,2,0:T(8,128)} %get-tuple-element.339, s32[]{:T(128)S(6)} %copy.85, f32[5,384,1152]{1,2,0:T(8,128)} %fusion.109, bf16[384,4,5,128]{0,3,2,1:T(8,128)(2,1)} %get-tuple-element.362, s32[]{:T(128)S(6)} %select_n.41), kind=kOutput, calls=%fused_computation.17.clone.clone.1 | convolution fusion | flops 568442880 | bytes 9928712 | tf_op jit(solution)/shard_map/while/body/eval_jaxpr/rts,trd->sd/dot_general | solution.py:56
  87.5 9.5 %fusion.109 = f32[5,384,1152]{1,2,0:T(8,128)} fusion(pred[384,1152]{0,1:T(8,128)(4,1)} %compare_and_fusion.3, bf16[384,4,5,128]{0,3,2,1:T(8,128)(2,1)} %get-tuple-element.360, s32[]{:T(128)S(6)} %select_n.41, bf16[1152,1,128]{2,1,0:T(2,128)(2,1)S(1)} %get-tuple-element.316), kind=kOutput, calls=%fused_computation.4.clone.clone.1 | convolution fusion | flops 1143524352 | bytes 11895808 | tf_op jit(solution)/shard_map/while/body/eval_jaxpr/reduce_sum | solution.py:45
  97.0 5.9 %fusion.113 = f32[4,1152,128]{1,2,0:T(8,128)} fusion(f32[4,1152,128]{1,2,0:T(8,128)} %get-tuple-element.339, s32[]{:T(128)S(6)} %copy.85, f32[5,384,1152]{1,2,0:T(8,128)} %fusion.109, bf16[384,4,5,128]{0,3,2,1:T(8,128)(2,1)} %get-tuple-element.362, s32[]{:T(128)S(6)} %select_n.41), kind=kOutput, calls=%fused_computation.17.clone.clone.1 | convolution fusion | flops 568442880 | bytes 9928712 | tf_op jit(solution)/shard_map/while/body/eval_jaxpr/rts,trd->sd/dot_general | solution.py:56
  117.8 9.4 %fusion.109 = f32[5,384,1152]{1,2,0:T(8,128)} fusion(pred[384,1152]{0,1:T(8,128)(4,1)} %compare_and_fusion.3, bf16[384,4,5,128]{0,3,2,1:T(8,128)(2,1)} %get-tuple-element.360, s32[]{:T(128)S(6)} %select_n.41, bf16[1152,1,128]{2,1,0:T(2,128)(2,1)S(1)} %get-tuple-element.316), kind=kOutput, calls=%fused_computation.4.clone.clone.1 | convolution fusion | flops 1143524352 | bytes 11895808 | tf_op jit(solution)/shard_map/while/body/eval_jaxpr/reduce_sum | solution.py:45
  127.2 5.9 %fusion.113 = f32[4,1152,128]{1,2,0:T(8,128)} fusion(f32[4,1152,128]{1,2,0:T(8,128)} %get-tuple-element.339, s32[]{:T(128)S(6)} %copy.85, f32[5,384,1152]{1,2,0:T(8,128)} %fusion.109, bf16[384,4,5,128]{0,3,2,1:T(8,128)(2,1)} %get-tuple-element.362, s32[]{:T(128)S(6)} %select_n.41), kind=kOutput, calls=%fused_computation.17.clone.clone.1 | convolution fusion | flops 568442880 | bytes 9928712 | tf_op jit(solution)/shard_map/while/body/eval_jaxpr/rts,trd->sd/dot_general | solution.py:56
  148.0 9.5 %fusion.109 = f32[5,384,1152]{1,2,0:T(8,128)} fusion(pred[384,1152]{0,1:T(8,128)(4,1)} %compare_and_fusion.3, bf16[384,4,5,128]{0,3,2,1:T(8,128)(2,1)} %get-tuple-element.360, s32[]{:T(128)S(6)} %select_n.41, bf16[1152,1,128]{2,1,0:T(2,128)(2,1)S(1)} %get-tuple-element.316), kind=kOutput, calls=%fused_computation.4.clone.clone.1 | convolution fusion | flops 1143524352 | bytes 11895808 | tf_op jit(solution)/shard_map/while/body/eval_jaxpr/reduce_sum | solution.py:45
  157.5 5.9 %fusion.113 = f32[4,1152,128]{1,2,0:T(8,128)} fusion(f32[4,1152,128]{1,2,0:T(8,128)} %get-tuple-element.339, s32[]{:T(128)S(6)} %copy.85, f32[5,384,1152]{1,2,0:T(8,128)} %fusion.109, bf16[384,4,5,128]{0,3,2,1:T(8,128)(2,1)} %get-tuple-element.362, s32[]{:T(128)S(6)} %select_n.41), kind=kOutput, calls=%fused_computation.17.clone.clone.1 | convolution fusion | flops 568442880 | bytes 9928712 | tf_op jit(solution)/shard_map/while/body/eval_jaxpr/rts,trd->sd/dot_general | solution.py:56
  182.5 5.3 %collective-permute-done.5 = bf16[384,512]{0,1:T(8,128)(2,1)S(1)} collective-permute-done((bf16[384,512]{0,1:T(8,128)(2,1)S(1)}, bf16[384,512]{0,1:T(8,128)(2,1)S(1)}, u32[]{:S(2)}, u32[]{:S(2)}) %collective-permute-start.5) | collective-permute-done | bytes 393248 | tf_op jit(solution)/shard_map/ppermute | solution.py:18
  187.8 5.3 %collective-permute-done.4 = bf16[384,512]{0,1:T(8,128)(2,1)S(1)} collective-permute-done((bf16[384,512]{0,1:T(8,128)(2,1)S(1)}, bf16[384,512]{0,1:T(8,128)(2,1)S(1)}, u32[]{:S(2)}, u32[]{:S(2)}) %collective-permute-start.4) | collective-permute-done | bytes 393248 | tf_op jit(solution)/shard_map/ppermute | solution.py:18
  193.4 11.3 %collective-permute-done.7 = bf16[384,512]{0,1:T(8,128)(2,1)S(1)} collective-permute-done((bf16[384,512]{0,1:T(8,128)(2,1)S(1)}, bf16[384,512]{0,1:T(8,128)(2,1)S(1)}, u32[]{:S(2)}, u32[]{:S(2)}) %collective-permute-start.7) | collective-permute-done | bytes 393248 | tf_op jit(solution)/shard_map/ppermute | solution.py:18
  204.8 6.3 %fusion.56 = f32[1024,2560]{1,0:T(8,128)} fusion(bf16[1,384,2560]{2,1,0:T(8,128)(2,1)S(1)} %copy-done, bf16[384,512]{0,1:T(8,128)(2,1)S(1)} %fusion.62, bf16[384,512]{0,1:T(8,128)(2,1)S(1)} %bitcast.188), kind=kOutput, calls=%fused_computation.53 | convolution fusion | flops 2014838784 | bytes 13238272 | tf_op jit(solution)/shard_map/dot_general | solution.py:149
  211.1 11.4 %copy.41 = f32[2560,2,512]{2,0,1:T(8,128)} copy(f32[2560,2,512]{0,2,1:T(8,128)} %bitcast.179) | data formatting | bytes 20971520 | tf_op jit(solution)/shard_map/reshape | solution.py:153
  222.6 184.5 %reduce-scatter.3.cloned.1.call-done = f32[320,2,512]{2,0,1:T(8,128)} async-done(((f32[2560,2,512]{2,0,1:T(8,128)}), f32[320,2,512]{2,0,1:T(8,128)}) %reduce-scatter.3.cloned.1.call-update) | async-done | bytes 1310736 | tf_op jit(solution)/shard_map/reduce_scatter | solution.py:152
  411.4 4.0 copy.42
  415.4 20.0 %reduce-scatter.5.cloned.1.call-done = f32[320,2,128]{2,0,1:T(8,128)} async-done(((f32[320,2,512]{2,0,1:T(8,128)}), f32[320,2,128]{2,0,1:T(8,128)}) %reduce-scatter.5.cloned.1.call-update) | async-done | bytes 327696 | tf_op jit(solution)/shard_map/reduce_scatter | solution.py:158
  (98 shorter events, 84.9 us)
Async XLA Ops:
  7.2 197.7 %copy-start = (bf16[1,384,2560]{2,1,0:T(8,128)(2,1)S(1)}, bf16[1,384,2560]{2,1,0:T(8,128)(2,1)}, u32[]{:S(2)}) copy-start(bf16[1,384,2560]{2,1,0:T(8,128)(2,1)} %param.14) | copy-start | bytes 5898244
  7.2 400.0 %reduce-scatter.3.cloned.1.call-start = ((), (), s32[]{:S(2)}) async-start(), calls=%async_computation.2 | async-start | bytes 11796480 | tf_op jit(solution)/shard_map/reduce_scatter | solution.py:152
  7.2 37.5 %collective-permute-start.1 = (bf16[384,512]{1,0:T(8,128)(2,1)}, bf16[384,512]{1,0:T(8,128)(2,1)}, u32[]{:S(2)}, u32[]{:S(2)}) collective-permute-start(bf16[384,512]{1,0:T(8,128)(2,1)} %bitcast.192), channel_id=1, source_target_pairs={{0,1},{1,2},{2,3},{3,4},{4,5},{5,6},{6,7},{8,9},{9,10},{10,11},{11... | collective-permute-start | bytes 1179656 | tf_op jit(solution)/shard_map/ppermute | solution.py:18
  13.0 31.7 %collective-permute-start = (bf16[384,512]{1,0:T(8,128)(2,1)}, bf16[384,512]{1,0:T(8,128)(2,1)}, u32[]{:S(2)}, u32[]{:S(2)}) collective-permute-start(bf16[384,512]{1,0:T(8,128)(2,1)} %bitcast.193), channel_id=1, source_target_pairs={{0,2},{1,3},{2,4},{3,5},{4,6},{5,7},{8,10},{9,11},{10,12},{11,13},... | collective-permute-start | bytes 1179656 | tf_op jit(solution)/shard_map/ppermute | solution.py:18
  16.5 24.9 %collective-permute-start.3 = (bf16[384,512]{1,0:T(8,128)(2,1)}, bf16[384,512]{1,0:T(8,128)(2,1)S(1)}, u32[]{:S(2)}, u32[]{:S(2)}) collective-permute-start(bf16[384,512]{1,0:T(8,128)(2,1)} %bitcast.189), channel_id=1, source_target_pairs={{0,1},{1,2},{2,3},{3,4},{4,5},{5,6},{6,7},{8,9},{9,10},{10,11},{11... | collective-permute-start | bytes 1179656 | tf_op jit(solution)/shard_map/ppermute | solution.py:18
  19.9 22.2 %collective-permute-start.2 = (bf16[384,512]{1,0:T(8,128)(2,1)}, bf16[384,512]{1,0:T(8,128)(2,1)}, u32[]{:S(2)}, u32[]{:S(2)}) collective-permute-start(bf16[384,512]{1,0:T(8,128)(2,1)} %bitcast.190), channel_id=1, source_target_pairs={{0,2},{1,3},{2,4},{3,5},{4,6},{5,7},{8,10},{9,11},{10,12},{11,13},... | collective-permute-start | bytes 1179656 | tf_op jit(solution)/shard_map/ppermute | solution.py:18
  36.3 5.9 %copy-start.3 = (bf16[1,384,512]{2,1,0:T(8,128)(2,1)S(1)}, bf16[1,384,512]{2,1,0:T(8,128)(2,1)}, u32[]{:S(2)}) copy-start(bf16[1,384,512]{2,1,0:T(8,128)(2,1)} %param.11) | copy-start | bytes 1179652
  41.4 0.7 copy-start.4
  43.4 3.7 copy-start.2
  66.7 6.3 %copy-start.1 = (f32[5,384,1152]{1,2,0:T(8,128)S(1)}, f32[5,384,1152]{1,2,0:T(8,128)}, u32[]{:S(2)}) copy-start(f32[5,384,1152]{1,2,0:T(8,128)} %fusion.109) | copy-start | bytes 26542084 | tf_op jit(solution)/shard_map/while
  97.0 6.3 %copy-start.1 = (f32[5,384,1152]{1,2,0:T(8,128)S(1)}, f32[5,384,1152]{1,2,0:T(8,128)}, u32[]{:S(2)}) copy-start(f32[5,384,1152]{1,2,0:T(8,128)} %fusion.109) | copy-start | bytes 26542084 | tf_op jit(solution)/shard_map/while
  127.2 6.3 %copy-start.1 = (f32[5,384,1152]{1,2,0:T(8,128)S(1)}, f32[5,384,1152]{1,2,0:T(8,128)}, u32[]{:S(2)}) copy-start(f32[5,384,1152]{1,2,0:T(8,128)} %fusion.109) | copy-start | bytes 26542084 | tf_op jit(solution)/shard_map/while
  157.5 6.3 %copy-start.1 = (f32[5,384,1152]{1,2,0:T(8,128)S(1)}, f32[5,384,1152]{1,2,0:T(8,128)}, u32[]{:S(2)}) copy-start(f32[5,384,1152]{1,2,0:T(8,128)} %fusion.109) | copy-start | bytes 26542084 | tf_op jit(solution)/shard_map/while
  171.6 5.4 %copy-start.5 = (f32[384]{0:T(512)S(1)}, f32[384]{0:T(512)}, u32[]{:S(2)}) copy-start(f32[384]{0:T(512)} %subtract_convert_fusion.2) | copy-start | bytes 4612
  171.6 5.4 %copy-start.6 = (f32[64]{0:T(128)S(1)}, f32[64]{0:T(128)}, u32[]{:S(2)}) copy-start(f32[64]{0:T(128)} %negate_power_fusion) | copy-start | bytes 772
  174.4 13.5 %collective-permute-start.5 = (bf16[384,512]{0,1:T(8,128)(2,1)S(1)}, bf16[384,512]{0,1:T(8,128)(2,1)S(1)}, u32[]{:S(2)}, u32[]{:S(2)}) collective-permute-start(bf16[384,512]{0,1:T(8,128)(2,1)S(1)} %bitcast.197), channel_id=1, source_target_pairs={{2,0},{3,1},{4,2},{5,3},{6,4},{7,5},{10,8},{11,9},{12,10},{13,11},... | collective-permute-start | bytes 1179656 | tf_op jit(solution)/shard_map/ppermute | solution.py:18
  175.7 17.5 %collective-permute-start.4 = (bf16[384,512]{0,1:T(8,128)(2,1)S(1)}, bf16[384,512]{0,1:T(8,128)(2,1)S(1)}, u32[]{:S(2)}, u32[]{:S(2)}) collective-permute-start(bf16[384,512]{0,1:T(8,128)(2,1)S(1)} %bitcast.195), channel_id=1, source_target_pairs={{1,0},{2,1},{3,2},{4,3},{5,4},{6,5},{7,6},{9,8},{10,9},{11,10},{12... | collective-permute-start | bytes 1179656 | tf_op jit(solution)/shard_map/ppermute | solution.py:18
  179.9 24.8 %collective-permute-start.7 = (bf16[384,512]{0,1:T(8,128)(2,1)S(1)}, bf16[384,512]{0,1:T(8,128)(2,1)S(1)}, u32[]{:S(2)}, u32[]{:S(2)}) collective-permute-start(bf16[384,512]{0,1:T(8,128)(2,1)S(1)} %bitcast.198), channel_id=1, source_target_pairs={{2,0},{3,1},{4,2},{5,3},{6,4},{7,5},{10,8},{11,9},{12,10},{13,11},... | collective-permute-start | bytes 1179656 | tf_op jit(solution)/shard_map/ppermute | solution.py:18
  181.2 23.5 %collective-permute-start.6 = (bf16[384,512]{0,1:T(8,128)(2,1)S(1)}, bf16[384,512]{0,1:T(8,128)(2,1)S(1)}, u32[]{:S(2)}, u32[]{:S(2)}) collective-permute-start(bf16[384,512]{0,1:T(8,128)(2,1)S(1)} %bitcast.196), channel_id=1, source_target_pairs={{1,0},{2,1},{3,2},{4,3},{5,4},{6,5},{7,6},{9,8},{10,9},{11,10},{12... | collective-permute-start | bytes 1179656 | tf_op jit(solution)/shard_map/ppermute | solution.py:18
  222.6 212.8 %reduce-scatter.5.cloned.1.call-start = ((), (), s32[]{:S(2)}) async-start(), calls=%async_computation.3 | async-start | bytes 1638400 | tf_op jit(solution)/shard_map/reduce_scatter | solution.py:158
Sparse Core Ops, SparseCore 0:
  222.7 184.4 reduce-scatter.2
  409.7 25.6 reduce-scatter.4
where the time goes:
time: 446 us; the launch traced here: 444 us
  waiting for transfers between devices  226 us (51%)
  matrix products  94.4 us (21%)
  local copies, waits for them, and re-layouts  58.3 us (13%)
  other arithmetic  22.1 us (5%)
  starting transfers between devices  21.4 us (5%)
  between operations  14.2 us (3%)
  loops' own time  6.98 us (2%)
    reduce_scatter x1, waiting for transfers between devices, on_device(): lax.psum_scatter(term.reshape(lax.axis_size('ctx') * row_count, 2, column...  185 us
    reduce_sum x4, matrix products, exp_totals(): jnp.sum(jnp.where(allowed[None], jnp.exp(logit_matrix), 0.0), axis=-1)  38 us
    dot_general x4, matrix products, group_grads(): jnp.einsum('rts,trd->sd', probability_narrow, d_group, preferred_element_...  23.7 us
    ppermute x8, waiting for transfers between devices, passed_along(): return lax.ppermute(x, axis, pairs)  21.9 us
    ppermute x8, starting transfers between devices, passed_along(): return lax.ppermute(x, axis, pairs)  21.3 us
    reduce_scatter x1, waiting for transfers between devices, on_device(): summed = lax.psum_scatter(summed, 'fsdp', scatter_dimension=2, tiled=True)  20 us
    unnamed x16, local copies, waits for them, and re-layouts  16.6 us
    reshape x1, local copies, waits for them, and re-layouts, on_device(): term.reshape(lax.axis_size('ctx') * row_count, 2, columns)  11.4 us
  transfers between devices with their start and end apart: 10, of which 5 were waited for; matrix products, arithmetic and copies ran while one was open for 7% of the time, Pallas kernels for 0%

commit v1 on v0

v1 whole, which is shorter than its diff:
```python
import math

import jax
import jax.numpy as jnp
from jax import lax
from jax.experimental import pallas as pl
from jax.experimental.pallas import tpu as pltpu
from jax.sharding import PartitionSpec as P

H = 20
G = 4
HD = 128
REP = H // G
DW = 2560
SPAN = 2
ROWS = 128
SCALE = 1.0 / math.sqrt(HD)
NT = (((1,), (1,)), ((), ()))


def passed_along(x, axis, by):
    peers = lax.axis_size(axis)
    pairs = [(i, i + by) for i in range(peers) if 0 <= i + by < peers]
    return lax.ppermute(x, axis, pairs)


def attention_kernel(
    start_ref, cos_ref, sin_ref, q_ref, o_ref, d_ref, k_ref, v_ref, near_ref, far_ref,
    dq_ref, own_ref, back1_ref, back2_ref,
    kwin, vwin, q_all, d_all, pt, dst, acc,
):
    step = pl.program_id(1)
    count = k_ref.shape[0]
    reach = SPAN * count
    window = reach + ROWS

    @pl.when(step == 0)
    def _():
        kwin[0:count] = far_ref[0]
        kwin[count : 2 * count] = near_ref[0]
        kwin[2 * count :] = k_ref[...]
        vwin[0:count] = far_ref[1]
        vwin[count : 2 * count] = near_ref[1]
        vwin[2 * count :] = v_ref[...]
        acc[...] = jnp.zeros_like(acc)

    first = pl.multiple_of(step * ROWS, ROWS)
    keys = kwin[pl.ds(first, window)]
    vals = vwin[pl.ds(first, window)]
    for j in range(REP):
        cols = slice(j * HD, (j + 1) * HD)
        rows = slice(j * ROWS, (j + 1) * ROWS)
        q_all[rows] = q_ref[:, cols]
        d_all[rows] = d_ref[:, cols]
    key_index = lax.broadcasted_iota(jnp.int32, (window, ROWS), 0)
    row_index = lax.broadcasted_iota(jnp.int32, (window, ROWS), 1)
    allowed = (key_index >= start_ref[...] - first) & (key_index <= row_index + reach)
    bias = jnp.where(allowed, 0.0, -1e30)
    scores = lax.dot_general(keys, q_all[...], NT, preferred_element_type=jnp.float32)
    gprobs = lax.dot_general(vals, d_all[...], NT, preferred_element_type=jnp.float32)
    for j in range(REP):
        cols = slice(j * HD, (j + 1) * HD)
        dots = jnp.sum(
            jnp.transpose(
                o_ref[:, cols].astype(jnp.float32) * d_ref[:, cols].astype(jnp.float32)
            ),
            axis=0,
            keepdims=True,
        )
        weights = jnp.exp2(scores[:, cols] * (SCALE * math.log2(math.e)) + bias)
        inverse = 1.0 / jnp.sum(weights, axis=0, keepdims=True)
        probs = weights * inverse
        pt[:, cols] = probs.astype(jnp.bfloat16)
        dst[:, cols] = (probs * (gprobs[:, cols] - dots)).astype(jnp.bfloat16)
    acc[1, pl.ds(first, window)] += jnp.dot(
        pt[...], d_all[...], preferred_element_type=jnp.float32
    )
    acc[0, pl.ds(first, window)] += jnp.dot(
        dst[...], q_all[...], preferred_element_type=jnp.float32
    )
    rot = jnp.dot(jnp.transpose(keys), dst[...], preferred_element_type=jnp.float32)
    half = HD // 2
    cosine = cos_ref[...] * SCALE
    sine = sin_ref[...] * SCALE
    for j in range(REP):
        cols = slice(j * HD, (j + 1) * HD)
        upper = rot[:half, cols]
        lower = rot[half:, cols]
        turned = jnp.concatenate(
            [upper * cosine + lower * sine, lower * cosine - upper * sine], axis=0
        )
        dq_ref[:, cols] = jnp.transpose(turned).astype(jnp.bfloat16)

    @pl.when(step == pl.num_programs(1) - 1)
    def _():
        for side, factor in ((0, SCALE), (1, 1.0)):
            back2_ref[side] = (acc[side, 0:count] * factor).astype(jnp.bfloat16)
            back1_ref[side] = (acc[side, count : 2 * count] * factor).astype(jnp.bfloat16)
            own_ref[side] = acc[side, 2 * count :] * factor


def attention(start, cos_t, sin_t, q, o, d, k, v, near, far):
    count = q.shape[0]
    steps = count // ROWS
    window = SPAN * count + ROWS
    half = HD // 2
    by_step = lambda g, i: (0, i)
    wide = pl.BlockSpec((ROWS, REP * HD), lambda g, i: (i, g))
    narrow = pl.BlockSpec((count, HD), lambda g, i: (0, g))
    pair = pl.BlockSpec((2, count, HD), lambda g, i: (0, 0, g))
    flops = G * steps * 5 * 2 * window * REP * ROWS * HD
    return pl.pallas_call(
        attention_kernel,
        grid=(G, steps),
        in_specs=[
            pl.BlockSpec((1, ROWS), by_step),
            pl.BlockSpec((half, ROWS), by_step),
            pl.BlockSpec((half, ROWS), by_step),
            wide, wide, wide, narrow, narrow, pair, pair,
        ],
        out_specs=[wide, pair, pair, pair],
        out_shape=[
            jax.ShapeDtypeStruct((count, H * HD), jnp.bfloat16),
            jax.ShapeDtypeStruct((2, count, G * HD), jnp.float32),
            jax.ShapeDtypeStruct((2, count, G * HD), jnp.bfloat16),
            jax.ShapeDtypeStruct((2, count, G * HD), jnp.bfloat16),
        ],
        scratch_shapes=[
            pltpu.VMEM(((SPAN + 1) * count, HD), jnp.bfloat16),
            pltpu.VMEM(((SPAN + 1) * count, HD), jnp.bfloat16),
            pltpu.VMEM((REP * ROWS, HD), jnp.bfloat16),
            pltpu.VMEM((REP * ROWS, HD), jnp.bfloat16),
            pltpu.VMEM((window, REP * ROWS), jnp.bfloat16),
            pltpu.VMEM((window, REP * ROWS), jnp.bfloat16),
            pltpu.VMEM((2, (SPAN + 1) * count, HD), jnp.float32),
        ],
        compiler_params=pltpu.CompilerParams(vmem_limit_bytes=48 << 20),
        cost_estimate=pl.CostEstimate(
            flops=2 * flops, bytes_accessed=16 << 20, transcendentals=steps * G * window * REP * ROWS
        ),
    )(start, cos_t, sin_t, q, o, d, k, v, near, far)


def on_device(queries, keys_rot, values, attention_out, grad_out, layer_input, doc_lengths):
    k_rows = keys_rot[0]
    v_rows = values[0]
    lengths = doc_lengths[0]
    count = k_rows.shape[0]
    shard = lax.axis_index("ctx")
    inputs = lax.all_gather(layer_input[0], "fsdp", axis=0, tiled=True)
    kv = jnp.stack([k_rows, v_rows])
    far = passed_along(kv, "ctx", 2)
    near = passed_along(kv, "ctx", 1)
    place = shard * count + jnp.arange(count, dtype=jnp.int32)
    starts = jnp.cumsum(lengths) - lengths
    start = jnp.max(jnp.where(starts[:, None] <= place[None, :], starts[:, None], 0), axis=0)
    local = (place - start).astype(jnp.float32)
    half = HD // 2
    inverse_freq = jnp.power(
        jnp.float32(1000000.0), -(jnp.arange(half, dtype=jnp.float32) * 2.0 / HD)
    )
    angles = inverse_freq[:, None] * local[None, :]
    cos_t = jnp.cos(angles)
    sin_t = jnp.sin(angles)
    relative = (start - (shard - SPAN) * count)[None, :]
    dq, own, back1, back2 = attention(
        relative, cos_t, sin_t, queries[0], attention_out[0], grad_out[0],
        k_rows, v_rows, near, far,
    )
    back2 = passed_along(back2, "ctx", -2)
    back1 = passed_along(back1, "ctx", -1)
    total = own + back1.astype(jnp.float32) + back2.astype(jnp.float32)
    heads = total[0].reshape(count, G, HD)
    cosine = cos_t.T[:, None, :]
    sine = sin_t.T[:, None, :]
    upper = heads[..., :half]
    lower = heads[..., half:]
    key_pre = jnp.concatenate(
        [upper * cosine + lower * sine, lower * cosine - upper * sine], axis=-1
    ).reshape(count, G * HD)
    both = jnp.stack([key_pre.astype(jnp.bfloat16), total[1].astype(jnp.bfloat16)])
    both = lax.all_to_all(both, "fsdp", split_axis=2, concat_axis=1, tiled=True)
    both = jnp.concatenate([both[0], both[1]], axis=1)
    term = lax.dot_general(
        inputs, both, (((0,), (0,)), ((), ())), preferred_element_type=jnp.float32
    )
    summed = lax.psum_scatter(term, "ctx", scatter_dimension=0, tiled=True)
    width = summed.shape[1] // 2
    return (dq[None], summed[:, :width], summed[:, width:])


def solution(mesh):
    in_specs = (
        P("fsdp", "ctx", None),
        P("fsdp", "ctx", None),
        P("fsdp", "ctx", None),
        P("fsdp", "ctx", None),
        P("fsdp", "ctx", None),
        P("fsdp", "ctx", None),
        P("fsdp", None),
    )
    out_specs = (P("fsdp", "ctx", None), P("ctx", "fsdp"), P("ctx", "fsdp"))
    return jax.shard_map(
        on_device, mesh=mesh, in_specs=in_specs, out_specs=out_specs, check_vma=False
    )
```

time: 446 us -> 217 us (0.49)
  waiting for transfers between devices: 226 us -> 135 us
  matrix products: 94.4 us -> 5.45 us
  local copies, waits for them, and re-layouts: 58.3 us -> 6.49 us
  Pallas kernels: 0 us -> 27.9 us
  other arithmetic: 22.1 us -> 3.01 us
  blocking collectives: 0 us -> 14.2 us
  starting transfers between devices: 21.4 us -> 11.1 us
  loops' own time: 6.98 us -> 0 us
    reduce_scatter x2 -> x0, waiting for transfers between devices: 205 us -> none  [the longest x1 185 us: on_device(): lax.psum_scatter(term.reshape(lax.axis_size('ctx') * row_count, 2, column...]
    unnamed x2 -> x3, waiting for transfers between devices: 0.03 us -> 70.5 us
    dot_general x17 -> x1, matrix products: 56.4 us -> 5.45 us  [on_device(): lax.dot_general(inputs, both, (((0,), (0,)), ((), ())), preferred_element...]
    ppermute x8 -> x4, waiting for transfers between devices: 21.9 us -> 64.1 us  [passed_along(): return lax.ppermute(x, axis, pairs)]
    reduce_sum x4 -> x0, matrix products: 38 us -> none  [exp_totals(): jnp.sum(jnp.where(allowed[None], jnp.exp(logit_matrix), 0.0), axis=-1)]
    pallas_call x0 -> x1, Pallas kernels: none -> 27.9 us  [attention(): pl.pallas_call(attention_kernel, grid=(G, steps), in_specs=[pl.BlockSpec(...]
    reshape x3 -> x0, local copies, waits for them, and re-layouts: 16.1 us -> none  [the longest x1 11.4 us: on_device(): term.reshape(lax.axis_size('ctx') * row_count, 2, columns)]
    all_to_all x0 -> x1, blocking collectives: none -> 14.2 us  [on_device(): both = lax.all_to_all(both, 'fsdp', split_axis=2, concat_axis=1, tiled=True)]
  transfers between devices with their start and end apart: 10 -> 6, of which waited for: 5 -> 5; matrix products, arithmetic and copies ran while one was open for 7% -> 2% of each run, Pallas kernels for 0% -> 13%
where the time goes in v1:
time: 217 us
  waiting for transfers between devices  135 us (62%)
  Pallas kernels  27.9 us (13%)
  between operations  14.3 us (7%)
  blocking collectives  14.2 us (7%)
  starting transfers between devices  11.1 us (5%)
  local copies, waits for them, and re-layouts  6.49 us (3%)
  matrix products  5.45 us (3%)
  other arithmetic  3.01 us (1%)
    unnamed x3, waiting for transfers between devices  70.5 us
    ppermute x4, waiting for transfers between devices, passed_along(): return lax.ppermute(x, axis, pairs)  64.1 us
    pallas_call x1, Pallas kernels, attention(): pl.pallas_call(attention_kernel, grid=(G, steps), in_specs=[pl.BlockSpec(...  27.9 us
    all_to_all x1, blocking collectives, on_device(): both = lax.all_to_all(both, 'fsdp', split_axis=2, concat_axis=1, tiled=True)  14.2 us
    ppermute x4, starting transfers between devices, passed_along(): return lax.ppermute(x, axis, pairs)  11 us
    dot_general x1, matrix products, on_device(): lax.dot_general(inputs, both, (((0,), (0,)), ((), ())), preferred_element...  5.45 us
  transfers between devices with their start and end apart: 6, of which 5 were waited for; matrix products, arithmetic and copies ran while one was open for 2% of the time, Pallas kernels for 13%

profile of v1, /device:TPU:0, one launch (start us, length us, event | category | flops | bytes accessed | tf_op | source)
XLA Modules:
  0.0 217.0 jit_solution(8589840508878158903)
XLA Ops:
  7.2 0.7 all-gather.3.cloned.1.call-update
  8.3 4.9 %collective-permute-start = (bf16[2,384,512]{2,1,0:T(8,128)(2,1)S(1)}, bf16[2,384,512]{2,1,0:T(8,128)(2,1)S(1)}, u32[]{:S(2)}, u32[]{:S(2)}) collective-permute-start(bf16[2,384,512]{2,1,0:T(8,128)(2,1)S(1)} %constant_dynamic-update-slice_fusion), channel_id=1, source_target_pairs={{0,1},{1,2},{2,3},{3,4},{4,5},{5,6},{6,7},{8,9},{9,10},{10,11},{11... | collective-permute-start | bytes 2359304 | tf_op jit(solution)/shard_map/ppermute | solution.py:24
  13.2 3.5 %collective-permute-start.1 = (bf16[2,384,512]{2,1,0:T(8,128)(2,1)S(1)}, bf16[2,384,512]{2,1,0:T(8,128)(2,1)S(1)}, u32[]{:S(2)}, u32[]{:S(2)}) collective-permute-start(bf16[2,384,512]{2,1,0:T(8,128)(2,1)S(1)} %constant_dynamic-update-slice_fusion), channel_id=1, source_target_pairs={{0,2},{1,3},{2,4},{3,5},{4,6},{5,7},{8,10},{9,11},{10,12},{11,13},... | collective-permute-start | bytes 2359304 | tf_op jit(solution)/shard_map/ppermute | solution.py:24
  17.1 0.4 multiply_sine_fusion.1
  17.5 12.5 %collective-permute-done.near_ref = bf16[2,384,512]{2,1,0:T(8,128)(2,1)S(1)} collective-permute-done((bf16[2,384,512]{2,1,0:T(8,128)(2,1)S(1)}, bf16[2,384,512]{2,1,0:T(8,128)(2,1)S(1)}, u32[]{:S(2)}, u32[]{:S(2)}) %collective-permute-start) | collective-permute-done | bytes 786464 | tf_op jit(solution)/shard_map/ppermute | solution.py:24
  30.0 3.2 %collective-permute-done.1.far_ref = bf16[2,384,512]{2,1,0:T(8,128)(2,1)S(1)} collective-permute-done((bf16[2,384,512]{2,1,0:T(8,128)(2,1)S(1)}, bf16[2,384,512]{2,1,0:T(8,128)(2,1)S(1)}, u32[]{:S(2)}, u32[]{:S(2)}) %collective-permute-start.1) | collective-permute-done | bytes 786464 | tf_op jit(solution)/shard_map/ppermute | solution.py:24
  33.2 27.9 %shard_map.94 = (bf16[384,2560]{1,0:T(8,128)(2,1)}, f32[2,384,512]{2,1,0:T(8,128)S(1)}, bf16[2,384,512]{2,1,0:T(8,128)(2,1)S(1)}, bf16[2,384,512]{2,1,0:T(8,128)(2,1)S(1)}) custom-call(s32[1,384]{1,0:T(1,128)S(1)} %sub.40.start_ref, f32[64,384]{1,0:T(8,128)S(1)} %get-tuple-element.35.cos_ref, f32[64,384]{1,0:T(8,128)S(1)} %get-tuple-element.34.sin_ref, ...), custom_call_target="tpu_custom_call" | custom-call | flops 17616076800 | bytes 16777216 | tf_op jit(solution)/shard_map/pallas_call | solution.py:112
  61.1 1.3 collective-permute-start.2
  62.4 1.3 collective-permute-start.3
  63.7 0.8 multiply_cosine_fusion
  64.4 30.4 %collective-permute-done.2 = bf16[2,384,512]{2,1,0:T(8,128)(2,1)S(1)} collective-permute-done((bf16[2,384,512]{2,1,0:T(8,128)(2,1)S(1)}, bf16[2,384,512]{2,1,0:T(8,128)(2,1)S(1)}, u32[]{:S(2)}, u32[]{:S(2)}) %collective-permute-start.2) | collective-permute-done | bytes 786464 | tf_op jit(solution)/shard_map/ppermute | solution.py:24
  94.8 18.0 %collective-permute-done.3 = bf16[2,384,512]{2,1,0:T(8,128)(2,1)S(1)} collective-permute-done((bf16[2,384,512]{2,1,0:T(8,128)(2,1)S(1)}, bf16[2,384,512]{2,1,0:T(8,128)(2,1)S(1)}, u32[]{:S(2)}, u32[]{:S(2)}) %collective-permute-start.3) | collective-permute-done | bytes 786464 | tf_op jit(solution)/shard_map/ppermute | solution.py:24
  112.8 0.3 convert_add_fusion
  113.2 0.3 reshape_squeeze.3
  113.5 0.6 add_convert_fusion
  114.2 0.5 pad_maximum_fusion.1
  114.9 1.1 copy.24
  116.1 14.2 %all_to_all.15 = bf16[2,384,512]{1,0,2:T(2,128)(2,1)S(1)} all-to-all(bf16[2,384,512]{1,0,2:T(2,128)(2,1)S(1)} %copy.24), channel_id=1, replica_groups=mesh['fsdp'=4,'ctx'=8] {'fsdp'}, dimensions={2} | all-to-all | bytes 1572864 | tf_op jit(solution)/shard_map/all_to_all | solution.py:182
  130.5 0.2 copy.26
  130.7 0.2 copy.27
  131.0 5.5 %fusion.2 = f32[2560,256]{0,1:T(8,128)S(1)} fusion(bf16[1,1536,2560]{2,1,0:T(8,128)(2,1)} %all-gather.3.cloned.1.call-done, bf16[1536,128]{1,0:T(8,128)(2,1)S(1)} %bitcast.28, bf16[1536,128]{1,0:T(8,128)(2,1)S(1)} %bitcast.27), kind=kOutput, calls=%fused_computation.2 | convolution fusion | flops 2014838784 | bytes 11272192 | tf_op jit(solution)/shard_map/dot_general | solution.py:184
  136.5 2.1 copy.30
  138.6 69.8 %reduce-scatter.4.cloned.1.call-done = f32[320,256]{1,0:T(8,128)} async-done(((f32[2560,256]{1,0:T(8,128)}), f32[320,256]{1,0:T(8,128)}) %reduce-scatter.4.cloned.1.call-update) | async-done | bytes 327696
  208.4 1.7 fusion.10
  (25 shorter events, 1.3 us)
Async XLA Ops:
  7.2 1.0 copy-start
  7.2 1.1 copy-start.1
  7.2 9.6 %copy-start.2 = (s32[1,7]{1,0:T(1,128)S(1)}, s32[1,7]{1,0:T(1,128)}, u32[]{:S(2)}) copy-start(s32[1,7]{1,0:T(1,128)} %param.13) | copy-start | bytes 88
  7.2 123.8 %all-gather.3.cloned.1.call-start = ((), (), s32[]{:S(2)}) async-start(), calls=%async_computation.2 | async-start | bytes 9830400 | tf_op jit(solution)/shard_map/all_gather | solution.py:150
  7.9 200.5 %reduce-scatter.4.cloned.1.call-start = ((), (), s32[]{:S(2)}) async-start(), calls=%async_computation.3 | async-start | bytes 2949120
  8.3 21.7 %collective-permute-start = (bf16[2,384,512]{2,1,0:T(8,128)(2,1)S(1)}, bf16[2,384,512]{2,1,0:T(8,128)(2,1)S(1)}, u32[]{:S(2)}, u32[]{:S(2)}) collective-permute-start(bf16[2,384,512]{2,1,0:T(8,128)(2,1)S(1)} %constant_dynamic-update-slice_fusion), channel_id=1, source_target_pairs={{0,1},{1,2},{2,3},{3,4},{4,5},{5,6},{6,7},{8,9},{9,10},{10,11},{11... | collective-permute-start | bytes 2359304 | tf_op jit(solution)/shard_map/ppermute | solution.py:24
  13.2 19.9 %collective-permute-start.1 = (bf16[2,384,512]{2,1,0:T(8,128)(2,1)S(1)}, bf16[2,384,512]{2,1,0:T(8,128)(2,1)S(1)}, u32[]{:S(2)}, u32[]{:S(2)}) collective-permute-start(bf16[2,384,512]{2,1,0:T(8,128)(2,1)S(1)} %constant_dynamic-update-slice_fusion), channel_id=1, source_target_pairs={{0,2},{1,3},{2,4},{3,5},{4,6},{5,7},{8,10},{9,11},{10,12},{11,13},... | collective-permute-start | bytes 2359304 | tf_op jit(solution)/shard_map/ppermute | solution.py:24
  61.1 33.7 %collective-permute-start.2 = (bf16[2,384,512]{2,1,0:T(8,128)(2,1)S(1)}, bf16[2,384,512]{2,1,0:T(8,128)(2,1)S(1)}, u32[]{:S(2)}, u32[]{:S(2)}) collective-permute-start(bf16[2,384,512]{2,1,0:T(8,128)(2,1)S(1)} %get-tuple-element.9), channel_id=1, source_target_pairs={{1,0},{2,1},{3,2},{4,3},{5,4},{6,5},{7,6},{9,8},{10,9},{11,10},{12... | collective-permute-start | bytes 2359304 | tf_op jit(solution)/shard_map/ppermute | solution.py:24
  62.4 50.5 %collective-permute-start.3 = (bf16[2,384,512]{2,1,0:T(8,128)(2,1)S(1)}, bf16[2,384,512]{2,1,0:T(8,128)(2,1)S(1)}, u32[]{:S(2)}, u32[]{:S(2)}) collective-permute-start(bf16[2,384,512]{2,1,0:T(8,128)(2,1)S(1)} %get-tuple-element.10), channel_id=1, source_target_pairs={{2,0},{3,1},{4,2},{5,3},{6,4},{7,5},{10,8},{11,9},{12,10},{13,11},... | collective-permute-start | bytes 2359304 | tf_op jit(solution)/shard_map/ppermute | solution.py:24
Sparse Core Ops, SparseCore 0:
  9.6 58.0 all-gather.2
  138.7 69.6 reduce-scatter.3

commit v2 on v1

--- a/solution.py
+++ b/solution.py
@@ -141,6 +141,92 @@
     )(start, cos_t, sin_t, q, o, d, k, v, near, far)
 
 
+def reduce_kernel(
+    term_ref, out_ref, paired, mine, got, send_one, recv_one, send_two, recv_two
+):
+    peers = term_ref.shape[0]
+    half = peers // 2
+    me = lax.axis_index("ctx")
+    parity = lax.rem(me, 2)
+    spot = lax.div(me, 2)
+    pair = me + 1 - 2 * parity
+    barrier = pltpu.get_barrier_semaphore()
+    pl.semaphore_signal(
+        barrier, inc=1, device_id={"ctx": pair}, device_id_type=pl.DeviceIdType.MESH
+    )
+    for k in range(half - 1):
+        other = 2 * lax.rem(spot + k + 1, half) + parity
+        pl.semaphore_signal(
+            barrier, inc=1, device_id={"ctx": other}, device_id_type=pl.DeviceIdType.MESH
+        )
+    pl.semaphore_wait(barrier, half)
+    firsts = []
+    for k in range(half):
+        target = lax.rem(spot + k + 1, half)
+        copy = pltpu.make_async_remote_copy(
+            src_ref=term_ref.at[2 * target + 1 - parity],
+            dst_ref=paired.at[k],
+            send_sem=send_one.at[k],
+            recv_sem=recv_one.at[k],
+            device_id={"ctx": pair},
+            device_id_type=pl.DeviceIdType.MESH,
+        )
+        copy.start()
+        firsts.append(copy)
+    seconds = []
+    total = None
+    for k in range(half):
+        target = lax.rem(spot + k + 1, half)
+        firsts[k].wait_recv()
+        summed = term_ref[2 * target + parity].astype(jnp.float32) + paired[k].astype(
+            jnp.float32
+        )
+        if k == half - 1:
+            out_ref[...] = summed
+            break
+        mine[k] = summed.astype(jnp.bfloat16)
+        copy = pltpu.make_async_remote_copy(
+            src_ref=mine.at[k],
+            dst_ref=got.at[k],
+            send_sem=send_two.at[k],
+            recv_sem=recv_two.at[k],
+            device_id={"ctx": 2 * target + parity},
+            device_id_type=pl.DeviceIdType.MESH,
+        )
+        copy.start()
+        seconds.append(copy)
+    for copy in seconds:
+        copy.wait_recv()
+    total = out_ref[...]
+    for k in range(half - 1):
+        total = total + got[k].astype(jnp.float32)
+    out_ref[...] = total
+    for copy in firsts + seconds:
+        copy.wait_send()
+
+
+def reduced(term, peers):
+    rows, width = term.shape[0] // peers, term.shape[1]
+    half = peers // 2
+    whole = pl.BlockSpec(memory_space=pltpu.VMEM)
+    return pl.pallas_call(
+        reduce_kernel,
+        in_specs=[whole],
+        out_specs=whole,
+        out_shape=jax.ShapeDtypeStruct((rows, width), jnp.float32),
+        scratch_shapes=[
+            pltpu.VMEM((half, rows, width), jnp.bfloat16),
+            pltpu.VMEM((half - 1, rows, width), jnp.bfloat16),
+            pltpu.VMEM((half - 1, rows, width), jnp.bfloat16),
+            pltpu.SemaphoreType.DMA((half,)),
+            pltpu.SemaphoreType.DMA((half,)),
+            pltpu.SemaphoreType.DMA((half - 1,)),
+            pltpu.SemaphoreType.DMA((half - 1,)),
+        ],
+        compiler_params=pltpu.CompilerParams(collective_id=1, has_side_effects=True),
+    )(term.reshape(peers, rows, width))
+
+
 def on_device(queries, keys_rot, values, attention_out, grad_out, layer_input, doc_lengths):
     k_rows = keys_rot[0]
     v_rows = values[0]
@@ -184,7 +270,7 @@
     term = lax.dot_general(
         inputs, both, (((0,), (0,)), ((), ())), preferred_element_type=jnp.float32
     )
-    summed = lax.psum_scatter(term, "ctx", scatter_dimension=0, tiled=True)
+    summed = reduced(term.astype(jnp.bfloat16), lax.axis_size("ctx"))
     width = summed.shape[1] // 2
     return (dq[None], summed[:, :width], summed[:, width:])
 

time: 217 us -> 171 us (0.79)
  waiting for transfers between devices: 135 us -> 64.8 us
  Pallas kernels: 27.9 us -> 51.8 us
    unnamed x3 -> x1, waiting for transfers between devices: 70.5 us -> 0.68 us
    pallas_call x0 -> x1, Pallas kernels: none -> 23.9 us  [reduced(): pl.pallas_call(reduce_kernel, in_specs=[whole], out_specs=whole, out_shap...]
  transfers between devices with their start and end apart: 6 -> 5, of which waited for: 5 -> 4; matrix products, arithmetic and copies ran while one was open for 2% -> 3% of each run, Pallas kernels for 13% -> 16%
where the time goes in v2:
time: 171 us; the launch traced here: 170 us
  waiting for transfers between devices  64.8 us (38%)
  Pallas kernels  51.8 us (30%)
  blocking collectives  14.2 us (8%)
  between operations  14.2 us (8%)
  starting transfers between devices  11 us (6%)
  local copies, waits for them, and re-layouts  5.88 us (3%)
  matrix products  5.45 us (3%)
  other arithmetic  3.01 us (2%)
    ppermute x4, waiting for transfers between devices, passed_along(): return lax.ppermute(x, axis, pairs)  64.1 us
    pallas_call x1, Pallas kernels, attention(): pl.pallas_call(attention_kernel, grid=(G, steps), in_specs=[pl.BlockSpec(...  27.9 us
    pallas_call x1, Pallas kernels, reduced(): pl.pallas_call(reduce_kernel, in_specs=[whole], out_specs=whole, out_shap...  23.9 us
    all_to_all x1, blocking collectives, on_device(): both = lax.all_to_all(both, 'fsdp', split_axis=2, concat_axis=1, tiled=True)  14.2 us
    ppermute x4, starting transfers between devices, passed_along(): return lax.ppermute(x, axis, pairs)  11 us
    dot_general x1, matrix products, on_device(): lax.dot_general(inputs, both, (((0,), (0,)), ((), ())), preferred_element...  5.45 us
  transfers between devices with their start and end apart: 5, of which 4 were waited for; matrix products, arithmetic and copies ran while one was open for 3% of the time, Pallas kernels for 16%

profile of v2, /device:TPU:0, one launch (start us, length us, event | category | flops | bytes accessed | tf_op | source)
XLA Modules:
  0.0 170.4 jit_solution(4279656994735359299)
XLA Ops:
  7.2 0.7 all-gather.3.cloned.1.call-update
  7.9 0.2 copy-done
  8.3 4.9 %collective-permute-start = (bf16[2,384,512]{2,1,0:T(8,128)(2,1)S(1)}, bf16[2,384,512]{2,1,0:T(8,128)(2,1)S(1)}, u32[]{:S(2)}, u32[]{:S(2)}) collective-permute-start(bf16[2,384,512]{2,1,0:T(8,128)(2,1)S(1)} %constant_dynamic-update-slice_fusion), channel_id=1, source_target_pairs={{0,1},{1,2},{2,3},{3,4},{4,5},{5,6},{6,7},{8,9},{9,10},{10,11},{11... | collective-permute-start | bytes 2359304 | tf_op jit(solution)/shard_map/ppermute | solution.py:24
  13.2 3.5 %collective-permute-start.1 = (bf16[2,384,512]{2,1,0:T(8,128)(2,1)S(1)}, bf16[2,384,512]{2,1,0:T(8,128)(2,1)S(1)}, u32[]{:S(2)}, u32[]{:S(2)}) collective-permute-start(bf16[2,384,512]{2,1,0:T(8,128)(2,1)S(1)} %constant_dynamic-update-slice_fusion), channel_id=1, source_target_pairs={{0,2},{1,3},{2,4},{3,5},{4,6},{5,7},{8,10},{9,11},{10,12},{11,13},... | collective-permute-start | bytes 2359304 | tf_op jit(solution)/shard_map/ppermute | solution.py:24
  17.1 0.4 multiply_sine_fusion.1
  17.5 12.5 %collective-permute-done.near_ref = bf16[2,384,512]{2,1,0:T(8,128)(2,1)S(1)} collective-permute-done((bf16[2,384,512]{2,1,0:T(8,128)(2,1)S(1)}, bf16[2,384,512]{2,1,0:T(8,128)(2,1)S(1)}, u32[]{:S(2)}, u32[]{:S(2)}) %collective-permute-start) | collective-permute-done | bytes 786464 | tf_op jit(solution)/shard_map/ppermute | solution.py:24
  30.0 3.2 %collective-permute-done.1.far_ref = bf16[2,384,512]{2,1,0:T(8,128)(2,1)S(1)} collective-permute-done((bf16[2,384,512]{2,1,0:T(8,128)(2,1)S(1)}, bf16[2,384,512]{2,1,0:T(8,128)(2,1)S(1)}, u32[]{:S(2)}, u32[]{:S(2)}) %collective-permute-start.1) | collective-permute-done | bytes 786464 | tf_op jit(solution)/shard_map/ppermute | solution.py:24
  33.2 27.9 %shard_map.94 = (bf16[384,2560]{1,0:T(8,128)(2,1)}, f32[2,384,512]{2,1,0:T(8,128)S(1)}, bf16[2,384,512]{2,1,0:T(8,128)(2,1)S(1)}, bf16[2,384,512]{2,1,0:T(8,128)(2,1)S(1)}) custom-call(s32[1,384]{1,0:T(1,128)S(1)} %sub.40.start_ref, f32[64,384]{1,0:T(8,128)S(1)} %get-tuple-element.20.cos_ref, f32[64,384]{1,0:T(8,128)S(1)} %get-tuple-element.19.sin_ref, ...), custom_call_target="tpu_custom_call" | custom-call | flops 17616076800 | bytes 16777216 | tf_op jit(solution)/shard_map/pallas_call | solution.py:112
  61.1 1.3 collective-permute-start.2
  62.4 1.3 collective-permute-start.3
  63.7 0.8 multiply_cosine_fusion
  64.4 30.4 %collective-permute-done.2 = bf16[2,384,512]{2,1,0:T(8,128)(2,1)S(1)} collective-permute-done((bf16[2,384,512]{2,1,0:T(8,128)(2,1)S(1)}, bf16[2,384,512]{2,1,0:T(8,128)(2,1)S(1)}, u32[]{:S(2)}, u32[]{:S(2)}) %collective-permute-start.2) | collective-permute-done | bytes 786464 | tf_op jit(solution)/shard_map/ppermute | solution.py:24
  94.8 18.0 %collective-permute-done.3 = bf16[2,384,512]{2,1,0:T(8,128)(2,1)S(1)} collective-permute-done((bf16[2,384,512]{2,1,0:T(8,128)(2,1)S(1)}, bf16[2,384,512]{2,1,0:T(8,128)(2,1)S(1)}, u32[]{:S(2)}, u32[]{:S(2)}) %collective-permute-start.3) | collective-permute-done | bytes 786464 | tf_op jit(solution)/shard_map/ppermute | solution.py:24
  112.8 0.3 convert_add_fusion
  113.2 0.3 reshape_squeeze.3
  113.5 0.6 add_convert_fusion
  114.2 0.5 pad_maximum_fusion.1
  114.9 1.1 copy.20
  116.1 14.2 %all_to_all.15 = bf16[2,384,512]{1,0,2:T(2,128)(2,1)S(1)} all-to-all(bf16[2,384,512]{1,0,2:T(2,128)(2,1)S(1)} %copy.20), channel_id=1, replica_groups=mesh['fsdp'=4,'ctx'=8] {'fsdp'}, dimensions={2} | all-to-all | bytes 1572864 | tf_op jit(solution)/shard_map/all_to_all | solution.py:268
  130.7 0.2 copy.23
  131.0 5.5 %fusion.5 = bf16[2560,256]{0,1:T(8,128)(2,1)S(1)} fusion(bf16[1,1536,2560]{2,1,0:T(8,128)(2,1)} %all-gather.3.cloned.1.call-done, bf16[1536,128]{1,0:T(8,128)(2,1)S(1)} %bitcast.31, bf16[1536,128]{1,0:T(8,128)(2,1)S(1)} %bitcast.30), kind=kOutput, calls=%fused_computation.3 | convolution fusion | flops 2015494144 | bytes 9961472 | tf_op jit(solution)/shard_map/dot_general | solution.py:270
  136.5 1.5 copy.24
  137.9 23.9 %shard_map.95 = f32[320,256]{1,0:T(8,128)} custom-call(bf16[8,320,256]{2,1,0:T(8,128)(2,1)} %bitcast.28), custom_call_target="tpu_custom_call" | custom-call | tf_op jit(solution)/shard_map/pallas_call | solution.py:212
  161.8 1.7 %fusion.13 = (f32[320,128]{1,0:T(8,128)}, f32[320,128]{1,0:T(8,128)}) fusion(f32[320,256]{1,0:T(8,128)} %shard_map.95), kind=kLoop, calls=%fused_computation.27 | loop fusion | bytes 655360 | tf_op jit(solution)/shard_map/slice | solution.py:275
  (23 shorter events, 1.3 us)
Async XLA Ops:
  7.2 1.0 copy-start
  7.2 1.1 copy-start.1
  7.2 9.6 %copy-start.2 = (s32[1,7]{1,0:T(1,128)S(1)}, s32[1,7]{1,0:T(1,128)}, u32[]{:S(2)}) copy-start(s32[1,7]{1,0:T(1,128)} %param.13) | copy-start | bytes 88
  7.2 123.8 %all-gather.3.cloned.1.call-start = ((), (), s32[]{:S(2)}) async-start(), calls=%async_computation.1 | async-start | bytes 9830400 | tf_op jit(solution)/shard_map/all_gather | solution.py:236
  8.3 21.7 %collective-permute-start = (bf16[2,384,512]{2,1,0:T(8,128)(2,1)S(1)}, bf16[2,384,512]{2,1,0:T(8,128)(2,1)S(1)}, u32[]{:S(2)}, u32[]{:S(2)}) collective-permute-start(bf16[2,384,512]{2,1,0:T(8,128)(2,1)S(1)} %constant_dynamic-update-slice_fusion), channel_id=1, source_target_pairs={{0,1},{1,2},{2,3},{3,4},{4,5},{5,6},{6,7},{8,9},{9,10},{10,11},{11... | collective-permute-start | bytes 2359304 | tf_op jit(solution)/shard_map/ppermute | solution.py:24
  13.2 19.9 %collective-permute-start.1 = (bf16[2,384,512]{2,1,0:T(8,128)(2,1)S(1)}, bf16[2,384,512]{2,1,0:T(8,128)(2,1)S(1)}, u32[]{:S(2)}, u32[]{:S(2)}) collective-permute-start(bf16[2,384,512]{2,1,0:T(8,128)(2,1)S(1)} %constant_dynamic-update-slice_fusion), channel_id=1, source_target_pairs={{0,2},{1,3},{2,4},{3,5},{4,6},{5,7},{8,10},{9,11},{10,12},{11,13},... | collective-permute-start | bytes 2359304 | tf_op jit(solution)/shard_map/ppermute | solution.py:24
  61.1 33.7 %collective-permute-start.2 = (bf16[2,384,512]{2,1,0:T(8,128)(2,1)S(1)}, bf16[2,384,512]{2,1,0:T(8,128)(2,1)S(1)}, u32[]{:S(2)}, u32[]{:S(2)}) collective-permute-start(bf16[2,384,512]{2,1,0:T(8,128)(2,1)S(1)} %get-tuple-element.9), channel_id=1, source_target_pairs={{1,0},{2,1},{3,2},{4,3},{5,4},{6,5},{7,6},{9,8},{10,9},{11,10},{12... | collective-permute-start | bytes 2359304 | tf_op jit(solution)/shard_map/ppermute | solution.py:24
  62.4 50.5 %collective-permute-start.3 = (bf16[2,384,512]{2,1,0:T(8,128)(2,1)S(1)}, bf16[2,384,512]{2,1,0:T(8,128)(2,1)S(1)}, u32[]{:S(2)}, u32[]{:S(2)}) collective-permute-start(bf16[2,384,512]{2,1,0:T(8,128)(2,1)S(1)} %get-tuple-element.10), channel_id=1, source_target_pairs={{2,0},{3,1},{4,2},{5,3},{6,4},{7,5},{10,8},{11,9},{12,10},{13,11},... | collective-permute-start | bytes 2359304 | tf_op jit(solution)/shard_map/ppermute | solution.py:24
Sparse Core Ops, SparseCore 0:
  9.6 58.0 all-gather.2

commit v3 on v2

--- a/solution.py
+++ b/solution.py
@@ -18,31 +18,186 @@
 NT = (((1,), (1,)), ((), ()))
 
 
-def passed_along(x, axis, by):
-    peers = lax.axis_size(axis)
-    pairs = [(i, i + by) for i in range(peers) if 0 <= i + by < peers]
-    return lax.ppermute(x, axis, pairs)
-
-
 def attention_kernel(
-    start_ref, cos_ref, sin_ref, q_ref, o_ref, d_ref, k_ref, v_ref, near_ref, far_ref,
-    dq_ref, own_ref, back1_ref, back2_ref,
+    start_ref, cos_ref, sin_ref, key_cos_ref, key_sin_ref, q_ref, o_ref, d_ref, k_ref, v_ref,
+    dq_ref, both_ref,
     kwin, vwin, q_all, d_all, pt, dst, acc,
+    own_kv, far_kv, near_kv, pair_out, pair_in, back_out, back_in, own_acc, done_out, done_in,
+    far_sems, near_sems, pair_sems, back_sems, done_sems,
 ):
+    group = pl.program_id(0)
     step = pl.program_id(1)
     count = k_ref.shape[0]
     reach = SPAN * count
     window = reach + ROWS
-
-    @pl.when(step == 0)
+    peers = lax.axis_size("ctx")
+    seqs = lax.axis_size("fsdp")
+    me = lax.axis_index("ctx")
+    seq = lax.axis_index("fsdp")
+    odd = lax.rem(me, 2) == 1
+    even = lax.rem(me, 2) == 0
+    pair = me + 1 - 2 * lax.rem(me, 2)
+    has_before = me >= 2
+    has_after = me < peers - 2
+    first_step = step == 0
+    last_step = step == pl.num_programs(1) - 1
+
+    def remote(src, dst_buf, sems, index, where):
+        return pltpu.make_async_remote_copy(
+            src_ref=src,
+            dst_ref=dst_buf,
+            send_sem=sems.at[0, index],
+            recv_sem=sems.at[1, index],
+            device_id=where,
+            device_id_type=pl.DeviceIdType.MESH,
+        )
+
+    def far_copy(g):
+        return remote(own_kv.at[g], far_kv.at[g], far_sems, g, {"ctx": me + 2})
+
+    def near_own(g):
+        return remote(own_kv.at[g], near_kv.at[g], near_sems, g, {"ctx": pair})
+
+    def near_relay(g):
+        return remote(far_kv.at[g], near_kv.at[g], near_sems, g, {"ctx": pair})
+
+    def pair_copy(g):
+        return remote(pair_out.at[g], pair_in.at[g], pair_sems, g, {"ctx": pair})
+
+    def back_copy(g):
+        return remote(back_out.at[g], back_in.at[g], back_sems, g, {"ctx": me - 2})
+
+    def done_copy(g):
+        return pltpu.make_async_remote_copy(
+            src_ref=done_out.at[g],
+            dst_ref=done_in.at[seq],
+            send_sem=done_sems.at[0, g],
+            recv_sem=done_sems.at[1, seq],
+            device_id={"fsdp": g},
+            device_id_type=pl.DeviceIdType.MESH,
+        )
+
+    def done_arrival(f):
+        return pltpu.make_async_remote_copy(
+            src_ref=done_out.at[f],
+            dst_ref=done_in.at[f],
+            send_sem=done_sems.at[0, f],
+            recv_sem=done_sems.at[1, f],
+            device_id={"fsdp": f},
+            device_id_type=pl.DeviceIdType.MESH,
+        )
+
+    def relay_near(g):
+        far_copy(g).wait_recv()
+        near_relay(g).start()
+
+    def relay_back(g):
+        pair_copy(g).wait_recv()
+        back_out[g] = (
+            back_out[g].astype(jnp.float32) + pair_in[g].astype(jnp.float32)
+        ).astype(jnp.bfloat16)
+        back_copy(g).start()
+
+    def finish(g):
+        @pl.when(even)
+        def _():
+            pair_copy(g).wait_recv()
+            own_acc[g] += pair_in[g].astype(jnp.float32)
+
+        @pl.when(has_after)
+        def _():
+            back_copy(g).wait_recv()
+            own_acc[g] += back_in[g].astype(jnp.float32)
+
+        keyed = own_acc[g, 0]
+        turned = keyed * key_cos_ref[...] + pltpu.roll(keyed, HD // 2, 1) * key_sin_ref[...]
+        done_out[g, 0] = turned.astype(jnp.bfloat16)
+        done_out[g, 1] = own_acc[g, 1].astype(jnp.bfloat16)
+
+        @pl.when(seq != g)
+        def _():
+            done_copy(g).start()
+
+    @pl.when(first_step & (group == 0))
     def _():
-        kwin[0:count] = far_ref[0]
-        kwin[count : 2 * count] = near_ref[0]
-        kwin[2 * count :] = k_ref[...]
-        vwin[0:count] = far_ref[1]
-        vwin[count : 2 * count] = near_ref[1]
-        vwin[2 * count :] = v_ref[...]
+        barrier = pltpu.get_barrier_semaphore()
+
+        def greet(where):
+            pl.semaphore_signal(
+                barrier, inc=1, device_id=where, device_id_type=pl.DeviceIdType.MESH
+            )
+
+        greet({"ctx": pair})
+        for k in range(1, seqs):
+            greet({"fsdp": lax.rem(seq + k, seqs)})
+
+        @pl.when(has_after)
+        def _():
+            greet({"ctx": me + 2})
+
+        @pl.when(has_before)
+        def _():
+            greet({"ctx": me - 2})
+
+        for g in range(G):
+            own_kv[g, 0] = k_ref[:, g * HD : (g + 1) * HD]
+            own_kv[g, 1] = v_ref[:, g * HD : (g + 1) * HD]
+        @pl.when(has_after & has_before)
+        def _():
+            pl.semaphore_wait(barrier, seqs + 2)
+
+        @pl.when(jnp.logical_not(has_after & has_before))
+        def _():
+            pl.semaphore_wait(barrier, seqs + 1)
+
+        for g in range(G):
+
+            @pl.when(has_after)
+            def _():
+                far_copy(g).start()
+
+            @pl.when(even)
+            def _():
+                near_own(g).start()
+
+        @pl.when(odd & has_before)
+        def _():
+            relay_near(0)
+
+    @pl.when(first_step & odd & has_before & (group < G - 1))
+    def _():
+        relay_near(group + 1)
+
+    @pl.when(first_step)
+    def _():
+        kwin[2 * count :] = own_kv[group, 0]
+        vwin[2 * count :] = own_kv[group, 1]
         acc[...] = jnp.zeros_like(acc)
+
+        @pl.when(even & has_before)
+        def _():
+            far_copy(group).wait_recv()
+
+        @pl.when(has_before)
+        def _():
+            kwin[0:count] = far_kv[group, 0]
+            vwin[0:count] = far_kv[group, 1]
+
+        @pl.when(me < 2)
+        def _():
+            kwin[0:count] = jnp.zeros((count, HD), jnp.bfloat16)
+            vwin[0:count] = jnp.zeros((count, HD), jnp.bfloat16)
+
+        @pl.when(me >= 1)
+        def _():
+            near_own(group).wait_recv()
+            kwin[count : 2 * count] = near_kv[group, 0]
+            vwin[count : 2 * count] = near_kv[group, 1]
+
+        @pl.when(me < 1)
+        def _():
+            kwin[count : 2 * count] = jnp.zeros((count, HD), jnp.bfloat16)
+            vwin[count : 2 * count] = jnp.zeros((count, HD), jnp.bfloat16)
 
     first = pl.multiple_of(step * ROWS, ROWS)
     keys = kwin[pl.ds(first, window)]
@@ -91,24 +246,86 @@
         )
         dq_ref[:, cols] = jnp.transpose(turned).astype(jnp.bfloat16)
 
-    @pl.when(step == pl.num_programs(1) - 1)
+    @pl.when(last_step)
     def _():
         for side, factor in ((0, SCALE), (1, 1.0)):
-            back2_ref[side] = (acc[side, 0:count] * factor).astype(jnp.bfloat16)
-            back1_ref[side] = (acc[side, count : 2 * count] * factor).astype(jnp.bfloat16)
-            own_ref[side] = acc[side, 2 * count :] * factor
-
-
-def attention(start, cos_t, sin_t, q, o, d, k, v, near, far):
+            pair_out[group, side] = (acc[side, count : 2 * count] * factor).astype(jnp.bfloat16)
+            back_out[group, side] = (acc[side, 0:count] * factor).astype(jnp.bfloat16)
+            own_acc[group, side] = acc[side, 2 * count :] * factor
+
+        @pl.when(me >= 1)
+        def _():
+            pair_copy(group).start()
+
+        @pl.when(even & has_before)
+        def _():
+            back_copy(group).start()
+
+        @pl.when(odd & has_before & (group >= 1))
+        def _():
+            relay_back(group - 1)
+
+        @pl.when(group >= 2)
+        def _():
+            finish(group - 2)
+
+    @pl.when(last_step & (group == G - 1))
+    def _():
+        @pl.when(odd & has_before)
+        def _():
+            relay_back(G - 1)
+
+        finish(G - 2)
+        finish(G - 1)
+
+        for f in range(seqs):
+            rows = slice(f * count, (f + 1) * count)
+
+            @pl.when(seq == f)
+            def _():
+                both_ref[rows, 0:HD] = done_out[f, 0]
+                both_ref[rows, HD:] = done_out[f, 1]
+
+            @pl.when(seq != f)
+            def _():
+                done_arrival(f).wait_recv()
+                both_ref[rows, 0:HD] = done_in[f, 0]
+                both_ref[rows, HD:] = done_in[f, 1]
+                done_arrival(f).wait_send()
+
+        for g in range(G):
+
+            @pl.when(has_after)
+            def _():
+                far_copy(g).wait_send()
+
+            @pl.when(even | has_before)
+            def _():
+                near_own(g).wait_send()
+
+            @pl.when(me >= 1)
+            def _():
+                pair_copy(g).wait_send()
+
+            @pl.when(has_before)
+            def _():
+                back_copy(g).wait_send()
+
+
+def attention(start, cos_t, sin_t, key_cos, key_sin, q, o, d, k, v, seqs):
     count = q.shape[0]
     steps = count // ROWS
     window = SPAN * count + ROWS
     half = HD // 2
     by_step = lambda g, i: (0, i)
+    fixed = lambda g, i: (0, 0)
     wide = pl.BlockSpec((ROWS, REP * HD), lambda g, i: (i, g))
-    narrow = pl.BlockSpec((count, HD), lambda g, i: (0, g))
-    pair = pl.BlockSpec((2, count, HD), lambda g, i: (0, 0, g))
+    rows = pl.BlockSpec((count, G * HD), fixed)
+    table = pl.BlockSpec((count, HD), fixed)
     flops = G * steps * 5 * 2 * window * REP * ROWS * HD
+    slots = pltpu.VMEM((G, 2, count, HD), jnp.bfloat16)
+    sems = pltpu.SemaphoreType.DMA((2, G))
+    assert seqs == G
     return pl.pallas_call(
         attention_kernel,
         grid=(G, steps),
@@ -116,14 +333,12 @@
             pl.BlockSpec((1, ROWS), by_step),
             pl.BlockSpec((half, ROWS), by_step),
             pl.BlockSpec((half, ROWS), by_step),
-            wide, wide, wide, narrow, narrow, pair, pair,
+            table, table, wide, wide, wide, rows, rows,
         ],
-        out_specs=[wide, pair, pair, pair],
+        out_specs=[wide, pl.BlockSpec((seqs * count, 2 * HD), fixed)],
         out_shape=[
             jax.ShapeDtypeStruct((count, H * HD), jnp.bfloat16),
-            jax.ShapeDtypeStruct((2, count, G * HD), jnp.float32),
-            jax.ShapeDtypeStruct((2, count, G * HD), jnp.bfloat16),
-            jax.ShapeDtypeStruct((2, count, G * HD), jnp.bfloat16),
+            jax.ShapeDtypeStruct((seqs * count, 2 * HD), jnp.bfloat16),
         ],
         scratch_shapes=[
             pltpu.VMEM(((SPAN + 1) * count, HD), jnp.bfloat16),
@@ -133,12 +348,18 @@
             pltpu.VMEM((window, REP * ROWS), jnp.bfloat16),
             pltpu.VMEM((window, REP * ROWS), jnp.bfloat16),
             pltpu.VMEM((2, (SPAN + 1) * count, HD), jnp.float32),
+            slots, slots, slots, slots, slots, slots, slots,
+            pltpu.VMEM((G, 2, count, HD), jnp.float32),
+            slots, slots,
+            sems, sems, sems, sems, sems,
         ],
-        compiler_params=pltpu.CompilerParams(vmem_limit_bytes=48 << 20),
+        compiler_params=pltpu.CompilerParams(
+            vmem_limit_bytes=48 << 20, collective_id=0, has_side_effects=True
+        ),
         cost_estimate=pl.CostEstimate(
             flops=2 * flops, bytes_accessed=16 << 20, transcendentals=steps * G * window * REP * ROWS
         ),
-    )(start, cos_t, sin_t, q, o, d, k, v, near, far)
+    )(start, cos_t, sin_t, key_cos, key_sin, q, o, d, k, v)
 
 
 def reduce_kernel(
@@ -234,9 +455,6 @@
     count = k_rows.shape[0]
     shard = lax.axis_index("ctx")
     inputs = lax.all_gather(layer_input[0], "fsdp", axis=0, tiled=True)
-    kv = jnp.stack([k_rows, v_rows])
-    far = passed_along(kv, "ctx", 2)
-    near = passed_along(kv, "ctx", 1)
     place = shard * count + jnp.arange(count, dtype=jnp.int32)
     starts = jnp.cumsum(lengths) - lengths
     start = jnp.max(jnp.where(starts[:, None] <= place[None, :], starts[:, None], 0), axis=0)
@@ -249,24 +467,12 @@
     cos_t = jnp.cos(angles)
     sin_t = jnp.sin(angles)
     relative = (start - (shard - SPAN) * count)[None, :]
-    dq, own, back1, back2 = attention(
-        relative, cos_t, sin_t, queries[0], attention_out[0], grad_out[0],
-        k_rows, v_rows, near, far,
-    )
-    back2 = passed_along(back2, "ctx", -2)
-    back1 = passed_along(back1, "ctx", -1)
-    total = own + back1.astype(jnp.float32) + back2.astype(jnp.float32)
-    heads = total[0].reshape(count, G, HD)
-    cosine = cos_t.T[:, None, :]
-    sine = sin_t.T[:, None, :]
-    upper = heads[..., :half]
-    lower = heads[..., half:]
-    key_pre = jnp.concatenate(
-        [upper * cosine + lower * sine, lower * cosine - upper * sine], axis=-1
-    ).reshape(count, G * HD)
-    both = jnp.stack([key_pre.astype(jnp.bfloat16), total[1].astype(jnp.bfloat16)])
-    both = lax.all_to_all(both, "fsdp", split_axis=2, concat_axis=1, tiled=True)
-    both = jnp.concatenate([both[0], both[1]], axis=1)
+    key_cos = jnp.concatenate([cos_t.T, cos_t.T], axis=1)
+    key_sin = jnp.concatenate([sin_t.T, -sin_t.T], axis=1)
+    dq, both = attention(
+        relative, cos_t, sin_t, key_cos, key_sin, queries[0], attention_out[0], grad_out[0],
+        k_rows, v_rows, lax.axis_size("fsdp"),
+    )
     term = lax.dot_general(
         inputs, both, (((0,), (0,)), ((), ())), preferred_element_type=jnp.float32
     )

time: 171 us -> 121 us (0.71)
  waiting for transfers between devices: 64.8 us -> 4.43 us
  Pallas kernels: 51.8 us -> 87.3 us
  blocking collectives: 14.2 us -> 0 us
  starting transfers between devices: 11 us -> 0.04 us
    ppermute x4 -> x0, waiting for transfers between devices: 64.1 us -> none  [passed_along(): return lax.ppermute(x, axis, pairs)]
    pallas_call x1, Pallas kernels: 27.9 us -> 61.1 us  [attention(): pl.pallas_call(attention_kernel, grid=(G, steps), in_specs=[pl.BlockSpec(...]
    all_to_all x1 -> x0, blocking collectives: 14.2 us -> none  [on_device(): both = lax.all_to_all(both, 'fsdp', split_axis=2, concat_axis=1, tiled=True)]
    ppermute x4 -> x0, starting transfers between devices: 11 us -> none  [passed_along(): return lax.ppermute(x, axis, pairs)]
    all_gather x1, waiting for transfers between devices: 0.02 us -> 3.75 us  [on_device(): inputs = lax.all_gather(layer_input[0], 'fsdp', axis=0, tiled=True)]
    unnamed x7 -> x9, local copies, waits for them, and re-layouts: 0.36 us -> 2.82 us
    pallas_call x1, Pallas kernels: 23.9 us -> 26.2 us  [reduced(): pl.pallas_call(reduce_kernel, in_specs=[whole], out_specs=whole, out_shap...]
  transfers between devices with their start and end apart: 5 -> 1, of which waited for: 4 -> 1; matrix products, arithmetic and copies ran while one was open for 3% -> 1% of each run, Pallas kernels for 16% -> 50%
where the time goes in v3:
time: 121 us
  Pallas kernels  87.3 us (72%)
  between operations  14.1 us (12%)
  local copies, waits for them, and re-layouts  6.98 us (6%)
  matrix products  6.51 us (5%)
  waiting for transfers between devices  4.43 us (4%)
  other arithmetic  1.65 us (1%)
    pallas_call x1, Pallas kernels, attention(): pl.pallas_call(attention_kernel, grid=(G, steps), in_specs=[pl.BlockSpec(...  61.1 us
    pallas_call x1, Pallas kernels, reduced(): pl.pallas_call(reduce_kernel, in_specs=[whole], out_specs=whole, out_shap...  26.2 us
    dot_general x1, matrix products, on_device(): lax.dot_general(inputs, both, (((0,), (0,)), ((), ())), preferred_element...  6.51 us
    all_gather x1, waiting for transfers between devices, on_device(): inputs = lax.all_gather(layer_input[0], 'fsdp', axis=0, tiled=True)  3.75 us
    unnamed x9, local copies, waits for them, and re-layouts  2.82 us
  transfers between devices with their start and end apart: 1, of which 1 were waited for; matrix products, arithmetic and copies ran while one was open for 1% of the time, Pallas kernels for 50%

profile of v3, /device:TPU:0, one launch (start us, length us, event | category | flops | bytes accessed | tf_op | source)
XLA Modules:
  0.0 121.1 jit_solution(5005617748838863094)
XLA Ops:
  7.2 0.0 copy-start.3
  7.2 0.0 copy-start.1
  7.2 0.0 copy-start.2
  7.2 0.0 all-gather.3.cloned.1.call-start
  7.2 0.7 all-gather.3.cloned.1.call-update
  7.9 0.0 copy-done.3
  7.9 0.2 reduce-window.8
  8.1 0.1 select_reduce_fusion
  8.3 0.8 multiply_sine_fusion
  9.0 0.2 pad_maximum_fusion
  9.2 0.4 multiply_sine_fusion.1
  9.6 0.0 copy-done.1
  9.6 0.0 copy-done.2
  9.7 0.0 copy-start
  9.7 1.5 %copy-done = bf16[1,384,2560]{2,1,0:T(8,128)(2,1)S(1)} copy-done((bf16[1,384,2560]{2,1,0:T(8,128)(2,1)S(1)}, bf16[1,384,2560]{2,1,0:T(8,128)(2,1)}, u32[]{:S(2)}) %copy-start) | copy-done | bytes 1966104
  11.2 61.1 %shard_map.94 = (bf16[384,2560]{1,0:T(8,128)(2,1)S(1)}, bf16[1536,256]{1,0:T(8,128)(2,1)S(1)}) custom-call(s32[1,384]{1,0:T(1,128)S(1)} %sub.37.start_ref, f32[64,384]{1,0:T(8,128)S(1)} %get-tuple-element.13.cos_ref, f32[64,384]{1,0:T(8,128)S(1)} %get-tuple-element.12.sin_ref, f32[384,128]{1,0:T(8,128)S(1)} %get-tuple-element.16.key_cos_ref, ...), custom_call_target="tpu_custom_call" | custom-call | flops 17616076800 | bytes 16777216 | tf_op jit(solution)/shard_map/pallas_call | solution.py:329
  72.3 3.8 %all-gather.3.cloned.1.call-done = bf16[1,1536,2560]{2,1,0:T(8,128)(2,1)} async-done(((bf16[1,384,2560]{2,1,0:T(8,128)(2,1)}), bf16[1,1536,2560]{2,1,0:T(8,128)(2,1)}) %all-gather.3.cloned.1.call-update) | async-done | bytes 7864336 | tf_op jit(solution)/shard_map/all_gather | solution.py:457
  76.1 6.5 %fusion.5 = bf16[2560,256]{0,1:T(8,128)(2,1)} fusion(bf16[1536,256]{1,0:T(8,128)(2,1)S(1)} %get-tuple-element.6, bf16[1,1536,2560]{2,1,0:T(8,128)(2,1)} %all-gather.3.cloned.1.call-done), kind=kOutput, calls=%fused_computation.3 | convolution fusion | flops 2013921280 | bytes 9961472 | tf_op jit(solution)/shard_map/dot_general | solution.py:476
  82.6 2.4 %copy.11 = bf16[2560,256]{1,0:T(8,128)(2,1)} copy(bf16[2560,256]{0,1:T(8,128)(2,1)} %fusion.5) | data formatting | bytes 2621440 | tf_op jit(solution)/shard_map/convert_element_type | solution.py:479
  85.0 26.2 %shard_map.95 = f32[320,256]{1,0:T(8,128)} custom-call(bf16[8,320,256]{2,1,0:T(8,128)(2,1)} %bitcast.26), custom_call_target="tpu_custom_call" | custom-call | tf_op jit(solution)/shard_map/pallas_call | solution.py:433
  111.2 1.7 %fusion.9 = (f32[320,128]{1,0:T(8,128)}, f32[320,128]{1,0:T(8,128)}) fusion(f32[320,256]{1,0:T(8,128)} %shard_map.95), kind=kLoop, calls=%fused_computation.17 | loop fusion | bytes 655360 | tf_op jit(solution)/shard_map/slice | solution.py:481
  113.0 1.3 %copy.13 = bf16[1,384,2560]{2,1,0:T(8,128)(2,1)} copy(bf16[1,384,2560]{2,1,0:T(8,128)(2,1)S(1)} %bitcast.22) | data formatting | bytes 3932160
  (5 shorter events, 0.0 us)
Async XLA Ops:
  7.2 0.8 copy-start.3
  7.2 2.5 %copy-start.1 = (bf16[1,384,512]{2,1,0:T(8,128)(2,1)S(1)}, bf16[1,384,512]{2,1,0:T(8,128)(2,1)}, u32[]{:S(2)}) copy-start(bf16[1,384,512]{2,1,0:T(8,128)(2,1)} %param.8) | copy-start | bytes 1179652
  7.2 2.5 %copy-start.2 = (bf16[1,384,512]{2,1,0:T(8,128)(2,1)S(1)}, bf16[1,384,512]{2,1,0:T(8,128)(2,1)}, u32[]{:S(2)}) copy-start(bf16[1,384,512]{2,1,0:T(8,128)(2,1)} %param.9) | copy-start | bytes 1179652
  7.2 68.9 %all-gather.3.cloned.1.call-start = ((), (), s32[]{:S(2)}) async-start(), calls=%async_computation | async-start | bytes 9830400 | tf_op jit(solution)/shard_map/all_gather | solution.py:457
  9.7 1.5 %copy-start = (bf16[1,384,2560]{2,1,0:T(8,128)(2,1)S(1)}, bf16[1,384,2560]{2,1,0:T(8,128)(2,1)}, u32[]{:S(2)}) copy-start(bf16[1,384,2560]{2,1,0:T(8,128)(2,1)} %param.7) | copy-start | bytes 5898244
Sparse Core Ops, SparseCore 0:
  9.6 66.4 all-gather.2

commit v4 on v3

--- a/solution.py
+++ b/solution.py
@@ -448,6 +448,121 @@
     )(term.reshape(peers, rows, width))
 
 
+def product_kernel(
+    li_ref, both_ref, out_ref,
+    turned, li_buf, term_wide, term, paired, mine, got,
+    li_sems, send_one, recv_one, send_two, recv_two,
+):
+    half, _, rows, _ = term.shape
+    me = lax.axis_index("ctx")
+    parity = lax.rem(me, 2)
+    spot = lax.div(me, 2)
+    pair = me + 1 - 2 * parity
+    loads = []
+    for k in range(half):
+        target = lax.rem(spot + k + 1, half)
+        first = pl.multiple_of(target * (2 * rows), 128)
+        load = pltpu.make_async_copy(
+            li_ref.at[:, pl.ds(first, 2 * rows)], li_buf.at[k], li_sems.at[k]
+        )
+        load.start()
+        loads.append(load)
+    barrier = pltpu.get_barrier_semaphore()
+    pl.semaphore_signal(
+        barrier, inc=1, device_id={"ctx": pair}, device_id_type=pl.DeviceIdType.MESH
+    )
+    for k in range(half - 1):
+        other = 2 * lax.rem(spot + k + 1, half) + parity
+        pl.semaphore_signal(
+            barrier, inc=1, device_id={"ctx": other}, device_id_type=pl.DeviceIdType.MESH
+        )
+    turned[...] = jnp.transpose(both_ref[...])
+    pl.semaphore_wait(barrier, half)
+    firsts = []
+    seconds = []
+
+    def pass_on(k):
+        target = lax.rem(spot + k + 1, half)
+        firsts[k].wait_recv()
+        summed = term_wide[k, parity] + paired[k].astype(jnp.float32)
+        if k == half - 1:
+            out_ref[...] = summed
+            return
+        mine[k] = summed.astype(jnp.bfloat16)
+        copy = pltpu.make_async_remote_copy(
+            src_ref=mine.at[k],
+            dst_ref=got.at[k],
+            send_sem=send_two.at[k],
+            recv_sem=recv_two.at[k],
+            device_id={"ctx": 2 * target + parity},
+            device_id_type=pl.DeviceIdType.MESH,
+        )
+        copy.start()
+        seconds.append(copy)
+
+    for k in range(half):
+        loads[k].wait()
+        product = jnp.transpose(
+            jnp.dot(turned[...], li_buf[k], preferred_element_type=jnp.float32)
+        )
+        for side in range(2):
+            piece = product[side * rows : (side + 1) * rows]
+            term_wide[k, side] = piece
+            term[k, side] = piece.astype(jnp.bfloat16)
+        copy = pltpu.make_async_remote_copy(
+            src_ref=term.at[k, 1 - parity],
+            dst_ref=paired.at[k],
+            send_sem=send_one.at[k],
+            recv_sem=recv_one.at[k],
+            device_id={"ctx": pair},
+            device_id_type=pl.DeviceIdType.MESH,
+        )
+        copy.start()
+        firsts.append(copy)
+    for k in range(half):
+        pass_on(k)
+    for copy in seconds:
+        copy.wait_recv()
+    total = out_ref[...]
+    for k in range(half - 1):
+        total = total + got[k].astype(jnp.float32)
+    out_ref[...] = total
+    for copy in firsts + seconds:
+        copy.wait_send()
+
+
+def product_reduced(inputs, both, peers):
+    depth, width = both.shape
+    rows = inputs.shape[1] // peers
+    half = peers // 2
+    return pl.pallas_call(
+        product_kernel,
+        in_specs=[
+            pl.BlockSpec(memory_space=pl.ANY),
+            pl.BlockSpec(memory_space=pltpu.VMEM),
+        ],
+        out_specs=pl.BlockSpec(memory_space=pltpu.VMEM),
+        out_shape=jax.ShapeDtypeStruct((rows, width), jnp.float32),
+        scratch_shapes=[
+            pltpu.VMEM((width, depth), jnp.bfloat16),
+            pltpu.VMEM((half, depth, 2 * rows), jnp.bfloat16),
+            pltpu.VMEM((half, 2, rows, width), jnp.float32),
+            pltpu.VMEM((half, 2, rows, width), jnp.bfloat16),
+            pltpu.VMEM((half, rows, width), jnp.bfloat16),
+            pltpu.VMEM((half - 1, rows, width), jnp.bfloat16),
+            pltpu.VMEM((half - 1, rows, width), jnp.bfloat16),
+            pltpu.SemaphoreType.DMA((half,)),
+            pltpu.SemaphoreType.DMA((half,)),
+            pltpu.SemaphoreType.DMA((half,)),
+            pltpu.SemaphoreType.DMA((half - 1,)),
+            pltpu.SemaphoreType.DMA((half - 1,)),
+        ],
+        compiler_params=pltpu.CompilerParams(
+            vmem_limit_bytes=48 << 20, collective_id=1, has_side_effects=True
+        ),
+    )(inputs, both)
+
+
 def on_device(queries, keys_rot, values, attention_out, grad_out, layer_input, doc_lengths):
     k_rows = keys_rot[0]
     v_rows = values[0]
@@ -473,10 +588,14 @@
         relative, cos_t, sin_t, key_cos, key_sin, queries[0], attention_out[0], grad_out[0],
         k_rows, v_rows, lax.axis_size("fsdp"),
     )
-    term = lax.dot_general(
-        inputs, both, (((0,), (0,)), ((), ())), preferred_element_type=jnp.float32
-    )
-    summed = reduced(term.astype(jnp.bfloat16), lax.axis_size("ctx"))
+    peers = lax.axis_size("ctx")
+    if (2 * DW // peers) % 128 == 0:
+        summed = product_reduced(inputs, both, peers)
+    else:
+        term = lax.dot_general(
+            inputs, both, (((0,), (0,)), ((), ())), preferred_element_type=jnp.float32
+        )
+        summed = reduced(term.astype(jnp.bfloat16), peers)
     width = summed.shape[1] // 2
     return (dq[None], summed[:, :width], summed[:, width:])
 

time: 121 us -> 110 us (0.909)
  matrix products: 6.51 us -> 0 us
  local copies, waits for them, and re-layouts: 6.98 us -> 3.57 us
    dot_general x1 -> x0, matrix products: 6.51 us -> none  [on_device(): lax.dot_general(inputs, both, (((0,), (0,)), ((), ())), preferred_element...]
    convert_element_type x1 -> x0, local copies, waits for them, and re-layouts: 2.42 us -> none  [on_device(): summed = reduced(term.astype(jnp.bfloat16), lax.axis_size('ctx'))]
  transfers between devices with their start and end apart: 1 -> 1, of which waited for: 1 -> 1; matrix products, arithmetic and copies ran while one was open for 1% -> 2% of each run, Pallas kernels for 50% -> 56%
where the time goes in v4:
time: 110 us
  Pallas kernels  86.2 us (78%)
  between operations  14.1 us (13%)
  waiting for transfers between devices  4.43 us (4%)
  local copies, waits for them, and re-layouts  3.57 us (3%)
  other arithmetic  1.65 us (2%)
    pallas_call x1, Pallas kernels, attention(): pl.pallas_call(attention_kernel, grid=(G, steps), in_specs=[pl.BlockSpec(...  61.1 us
    pallas_call x1, Pallas kernels, product_reduced(): pl.pallas_call(product_kernel, in_specs=[pl.BlockSpec(memory_space=pl.ANY...  25.1 us
    all_gather x1, waiting for transfers between devices, on_device(): inputs = lax.all_gather(layer_input[0], 'fsdp', axis=0, tiled=True)  3.75 us
    unnamed x9, local copies, waits for them, and re-layouts  2.82 us
  transfers between devices with their start and end apart: 1, of which 1 were waited for; matrix products, arithmetic and copies ran while one was open for 2% of the time, Pallas kernels for 56%

profile of v4, /device:TPU:0, one launch (start us, length us, event | category | flops | bytes accessed | tf_op | source)
XLA Modules:
  0.0 110.0 jit_solution(13851530497155330681)
XLA Ops:
  7.2 0.0 copy-start.3
  7.2 0.0 copy-start.1
  7.2 0.0 copy-start.2
  7.2 0.0 all-gather.3.cloned.1.call-start
  7.2 0.7 all-gather.3.cloned.1.call-update
  7.9 0.0 copy-done.3
  7.9 0.2 reduce-window.8
  8.1 0.1 select_reduce_fusion
  8.3 0.8 multiply_sine_fusion
  9.0 0.2 pad_maximum_fusion
  9.2 0.4 multiply_sine_fusion.1
  9.6 0.0 copy-done.1
  9.6 0.0 copy-done.2
  9.7 0.0 copy-start
  9.7 1.5 %copy-done = bf16[1,384,2560]{2,1,0:T(8,128)(2,1)S(1)} copy-done((bf16[1,384,2560]{2,1,0:T(8,128)(2,1)S(1)}, bf16[1,384,2560]{2,1,0:T(8,128)(2,1)}, u32[]{:S(2)}) %copy-start) | copy-done | bytes 1966104
  11.2 61.1 %shard_map.94 = (bf16[384,2560]{1,0:T(8,128)(2,1)S(1)}, bf16[1536,256]{1,0:T(8,128)(2,1)S(1)}) custom-call(s32[1,384]{1,0:T(1,128)S(1)} %sub.37.start_ref, f32[64,384]{1,0:T(8,128)S(1)} %get-tuple-element.13.cos_ref, f32[64,384]{1,0:T(8,128)S(1)} %get-tuple-element.12.sin_ref, f32[384,128]{1,0:T(8,128)S(1)} %get-tuple-element.16.key_cos_ref, ...), custom_call_target="tpu_custom_call" | custom-call | flops 17616076800 | bytes 16777216 | tf_op jit(solution)/shard_map/pallas_call | solution.py:329
  72.3 3.8 %all-gather.3.cloned.1.call-done = bf16[1,1536,2560]{2,1,0:T(8,128)(2,1)} async-done(((bf16[1,384,2560]{2,1,0:T(8,128)(2,1)}), bf16[1,1536,2560]{2,1,0:T(8,128)(2,1)}) %all-gather.3.cloned.1.call-update) | async-done | bytes 7864336 | tf_op jit(solution)/shard_map/all_gather | solution.py:572
  76.1 25.1 %shard_map.95 = f32[320,256]{1,0:T(8,128)S(1)} custom-call(bf16[1536,2560]{1,0:T(8,128)(2,1)} %bitcast.16, bf16[1536,256]{1,0:T(8,128)(2,1)S(1)} %get-tuple-element.6.both_ref), custom_call_target="tpu_custom_call" | custom-call | tf_op jit(solution)/shard_map/pallas_call | solution.py:538
  101.1 0.7 fusion.1
  101.9 1.3 %copy.11 = bf16[1,384,2560]{2,1,0:T(8,128)(2,1)} copy(bf16[1,384,2560]{2,1,0:T(8,128)(2,1)S(1)} %bitcast.12) | data formatting | bytes 3932160
  (5 shorter events, 0.0 us)
Async XLA Ops:
  7.2 0.8 copy-start.3
  7.2 2.5 %copy-start.1 = (bf16[1,384,512]{2,1,0:T(8,128)(2,1)S(1)}, bf16[1,384,512]{2,1,0:T(8,128)(2,1)}, u32[]{:S(2)}) copy-start(bf16[1,384,512]{2,1,0:T(8,128)(2,1)} %param.8) | copy-start | bytes 1179652
  7.2 2.5 %copy-start.2 = (bf16[1,384,512]{2,1,0:T(8,128)(2,1)S(1)}, bf16[1,384,512]{2,1,0:T(8,128)(2,1)}, u32[]{:S(2)}) copy-start(bf16[1,384,512]{2,1,0:T(8,128)(2,1)} %param.9) | copy-start | bytes 1179652
  7.2 68.9 %all-gather.3.cloned.1.call-start = ((), (), s32[]{:S(2)}) async-start(), calls=%async_computation | async-start | bytes 9830400 | tf_op jit(solution)/shard_map/all_gather | solution.py:572
  9.7 1.5 %copy-start = (bf16[1,384,2560]{2,1,0:T(8,128)(2,1)S(1)}, bf16[1,384,2560]{2,1,0:T(8,128)(2,1)}, u32[]{:S(2)}) copy-start(bf16[1,384,2560]{2,1,0:T(8,128)(2,1)} %param.7) | copy-start | bytes 5898244
Sparse Core Ops, SparseCore 0:
  9.6 66.4 all-gather.2

commit v5 on v4

--- a/solution.py
+++ b/solution.py
@@ -19,11 +19,12 @@
 
 
 def attention_kernel(
-    start_ref, cos_ref, sin_ref, key_cos_ref, key_sin_ref, q_ref, o_ref, d_ref, k_ref, v_ref,
-    dq_ref, both_ref,
+    start_ref, cos_ref, sin_ref, key_cos_ref, key_sin_ref, q_ref, o_ref, d_ref, k_ref, v_ref, li_ref,
+    dq_ref, both_ref, li_all,
     kwin, vwin, q_all, d_all, pt, dst, acc,
     own_kv, far_kv, near_kv, pair_out, pair_in, back_out, back_in, own_acc, done_out, done_in,
-    far_sems, near_sems, pair_sems, back_sems, done_sems,
+    far_sems, near_sems, pair_sems, back_sems, done_sems, cross_sems, pass_sems, core_sems,
+    local_sem,
 ):
     group = pl.program_id(0)
     step = pl.program_id(1)
@@ -87,6 +88,30 @@
             device_id_type=pl.DeviceIdType.MESH,
         )
 
+    core = seq + 1 - 2 * lax.rem(seq, 2)
+    across = lax.rem(seq + 2, seqs)
+    piece = count // G
+
+    def core_copy():
+        return remote(li_ref, li_all.at[seq], core_sems, 0, {"fsdp": core})
+
+    def local_copy():
+        return pltpu.make_async_copy(li_ref, li_all.at[seq], local_sem)
+
+    def cross_copy(g):
+        rows = pl.ds(g * piece, piece)
+        return remote(
+            li_ref.at[rows], li_all.at[seq, rows], cross_sems, g, {"fsdp": across}
+        )
+
+    def pass_copy(g):
+        part = li_all.at[across, pl.ds(g * piece, piece)]
+        return remote(part, part, pass_sems, g, {"fsdp": core})
+
+    def pass_across(g):
+        cross_copy(g).wait_recv()
+        pass_copy(g).start()
+
     def relay_near(g):
         far_copy(g).wait_recv()
         near_relay(g).start()
@@ -159,6 +184,11 @@
             @pl.when(even)
             def _():
                 near_own(g).start()
+
+        for g in range(G):
+            cross_copy(g).start()
+        core_copy().start()
+        local_copy().start()
 
         @pl.when(odd & has_before)
         def _():
@@ -265,6 +295,10 @@
         def _():
             relay_back(group - 1)
 
+        @pl.when(group >= 1)
+        def _():
+            pass_across(group - 1)
+
         @pl.when(group >= 2)
         def _():
             finish(group - 2)
@@ -276,6 +310,7 @@
             relay_back(G - 1)
 
         finish(G - 2)
+        pass_across(G - 1)
         finish(G - 1)
 
         for f in range(seqs):
@@ -311,8 +346,14 @@
             def _():
                 back_copy(g).wait_send()
 
-
-def attention(start, cos_t, sin_t, key_cos, key_sin, q, o, d, k, v, seqs):
+            cross_copy(g).wait_send()
+            pass_copy(g).wait()
+
+        core_copy().wait()
+        local_copy().wait()
+
+
+def attention(start, cos_t, sin_t, key_cos, key_sin, q, o, d, k, v, li, seqs):
     count = q.shape[0]
     steps = count // ROWS
     window = SPAN * count + ROWS
@@ -334,11 +375,17 @@
             pl.BlockSpec((half, ROWS), by_step),
             pl.BlockSpec((half, ROWS), by_step),
             table, table, wide, wide, wide, rows, rows,
+            pl.BlockSpec(memory_space=pl.ANY),
         ],
-        out_specs=[wide, pl.BlockSpec((seqs * count, 2 * HD), fixed)],
+        out_specs=[
+            wide,
+            pl.BlockSpec((seqs * count, 2 * HD), fixed),
+            pl.BlockSpec(memory_space=pl.ANY),
+        ],
         out_shape=[
             jax.ShapeDtypeStruct((count, H * HD), jnp.bfloat16),
             jax.ShapeDtypeStruct((seqs * count, 2 * HD), jnp.bfloat16),
+            jax.ShapeDtypeStruct((seqs, count, li.shape[1]), li.dtype),
         ],
         scratch_shapes=[
             pltpu.VMEM(((SPAN + 1) * count, HD), jnp.bfloat16),
@@ -351,7 +398,9 @@
             slots, slots, slots, slots, slots, slots, slots,
             pltpu.VMEM((G, 2, count, HD), jnp.float32),
             slots, slots,
-            sems, sems, sems, sems, sems,
+            sems, sems, sems, sems, sems, sems, sems,
+            pltpu.SemaphoreType.DMA((2, 1)),
+            pltpu.SemaphoreType.DMA,
         ],
         compiler_params=pltpu.CompilerParams(
             vmem_limit_bytes=48 << 20, collective_id=0, has_side_effects=True
@@ -359,7 +408,7 @@
         cost_estimate=pl.CostEstimate(
             flops=2 * flops, bytes_accessed=16 << 20, transcendentals=steps * G * window * REP * ROWS
         ),
-    )(start, cos_t, sin_t, key_cos, key_sin, q, o, d, k, v)
+    )(start, cos_t, sin_t, key_cos, key_sin, q, o, d, k, v, li)
 
 
 def reduce_kernel(
@@ -569,7 +618,6 @@
     lengths = doc_lengths[0]
     count = k_rows.shape[0]
     shard = lax.axis_index("ctx")
-    inputs = lax.all_gather(layer_input[0], "fsdp", axis=0, tiled=True)
     place = shard * count + jnp.arange(count, dtype=jnp.int32)
     starts = jnp.cumsum(lengths) - lengths
     start = jnp.max(jnp.where(starts[:, None] <= place[None, :], starts[:, None], 0), axis=0)
@@ -584,10 +632,11 @@
     relative = (start - (shard - SPAN) * count)[None, :]
     key_cos = jnp.concatenate([cos_t.T, cos_t.T], axis=1)
     key_sin = jnp.concatenate([sin_t.T, -sin_t.T], axis=1)
-    dq, both = attention(
+    dq, both, inputs = attention(
         relative, cos_t, sin_t, key_cos, key_sin, queries[0], attention_out[0], grad_out[0],
-        k_rows, v_rows, lax.axis_size("fsdp"),
-    )
+        k_rows, v_rows, layer_input[0], lax.axis_size("fsdp"),
+    )
+    inputs = inputs.reshape(-1, DW)
     peers = lax.axis_size("ctx")
     if (2 * DW // peers) % 128 == 0:
         summed = product_reduced(inputs, both, peers)

time: 110 us -> 99.9 us (0.908)
  between operations: 14.1 us -> 0.7 us
  waiting for transfers between devices: 4.43 us -> 0 us
  Pallas kernels: 86.2 us -> 90.4 us
  local copies, waits for them, and re-layouts: 3.57 us -> 5.55 us
  other arithmetic: 1.65 us -> 2.95 us
    pallas_call x1, Pallas kernels: 61.1 us -> 65.3 us  [attention(): pl.pallas_call(attention_kernel, grid=(G, steps), in_specs=[pl.BlockSpec(...]
    all_gather x1 -> x0, waiting for transfers between devices: 3.75 us -> none  [on_device(): inputs = lax.all_gather(layer_input[0], 'fsdp', axis=0, tiled=True)]
    unnamed x9 -> x7, local copies, waits for them, and re-layouts: 2.82 us -> 4.8 us
  transfers between devices with their start and end apart: 1 -> 0, of which waited for: 1 -> 0; matrix products, arithmetic and copies ran while one was open for 2% -> 0% of each run, Pallas kernels for 56% -> 0%
where the time goes in v5:
time: 99.9 us; the launch traced here: 99.6 us
  Pallas kernels  90.4 us (90%)
  local copies, waits for them, and re-layouts  5.55 us (6%)
  other arithmetic  2.95 us (3%)
    pallas_call x1, Pallas kernels, attention(): pl.pallas_call(attention_kernel, grid=(G, steps), in_specs=[pl.BlockSpec(...  65.3 us
    pallas_call x1, Pallas kernels, product_reduced(): pl.pallas_call(product_kernel, in_specs=[pl.BlockSpec(memory_space=pl.ANY...  25.1 us
    unnamed x7, local copies, waits for them, and re-layouts  4.8 us

profile of v5, /device:TPU:0, one launch (start us, length us, event | category | flops | bytes accessed | tf_op | source)
XLA Modules:
  0.0 99.6 jit_solution(8308671821769661560)
XLA Ops:
  0.6 0.8 reduce-window.8
  1.5 0.7 bitcast_subtract_fusion
  2.1 0.1 select_reduce_fusion
  2.2 0.8 multiply_sine_fusion
  3.0 0.2 pad_maximum_fusion
  3.2 0.4 multiply_sine_fusion.1
  3.6 0.0 copy-start
  3.6 1.5 %copy-done = bf16[1,384,2560]{2,1,0:T(8,128)(2,1)S(1)} copy-done((bf16[1,384,2560]{2,1,0:T(8,128)(2,1)S(1)}, bf16[1,384,2560]{2,1,0:T(8,128)(2,1)}, u32[]{:S(2)}) %copy-start) | copy-done | bytes 1966104
  5.2 0.0 copy-start.1
  5.2 1.0 copy-done.1
  6.2 0.0 copy-start.2
  6.2 1.0 copy-done.2
  7.2 65.3 %shard_map.94 = (bf16[384,2560]{1,0:T(8,128)(2,1)S(1)}, bf16[1536,256]{1,0:T(8,128)(2,1)S(1)}, bf16[4,384,2560]{2,1,0:T(8,128)(2,1)}) custom-call(s32[1,384]{1,0:T(1,128)S(1)} %sub.37.start_ref, f32[64,384]{1,0:T(8,128)S(1)} %get-tuple-element.15.cos_ref, f32[64,384]{1,0:T(8,128)S(1)} %get-tuple-element.14.sin_ref, ...), custom_call_target="tpu_custom_call" | custom-call | flops 17616076800 | bytes 16777216 | tf_op jit(solution)/shard_map/pallas_call | solution.py:370
  72.5 25.1 %shard_map.95 = f32[320,256]{1,0:T(8,128)S(1)} custom-call(bf16[1536,2560]{1,0:T(8,128)(2,1)} %bitcast.17, bf16[1536,256]{1,0:T(8,128)(2,1)S(1)} %get-tuple-element.8.both_ref), custom_call_target="tpu_custom_call" | custom-call | tf_op jit(solution)/shard_map/pallas_call | solution.py:587
  97.6 0.7 fusion.1
  98.3 1.3 %copy.11 = bf16[1,384,2560]{2,1,0:T(8,128)(2,1)} copy(bf16[1,384,2560]{2,1,0:T(8,128)(2,1)S(1)} %bitcast.13) | data formatting | bytes 3932160
  (4 shorter events, 0.0 us)
Async XLA Ops:
  3.6 1.5 %copy-start = (bf16[1,384,2560]{2,1,0:T(8,128)(2,1)S(1)}, bf16[1,384,2560]{2,1,0:T(8,128)(2,1)}, u32[]{:S(2)}) copy-start(bf16[1,384,2560]{2,1,0:T(8,128)(2,1)} %param.7) | copy-start | bytes 5898244
  5.2 1.0 copy-start.1
  6.2 1.0 copy-start.2
